TPU v7x, 32 devices: a whole 2x2x4 slice. The times are simulated.
32 devices in a mesh: groups: 2 (over y), geom: 4 (over z), design: 2 (over x), head: 2 (over core).
Axes of the slice: x: 2, y: 2, z: 4, core: 2. Of those that a mesh axis runs over, the one named last changes fastest.
Arguments:
- point_feats: bfloat16 [4, 12288, 192], P(('groups', 'design'), ('geom', 'head')), parts along dimension 0, may hold values from -6 to 6
- block_anchor: int32 [4, 96], P(('groups', 'design'), ('geom', 'head')), parts along dimension 0, may hold values from 0 to 127, as said below
- anchor_feats: bfloat16 [4, 128, 192], P(('groups', 'design'), ('geom', 'head')), parts along dimension 0, may hold values from -4 to 4
- query_feats: bfloat16 [4, 4096, 192], P(('groups', 'design'), ('geom', 'head')), parts along dimension 0, may hold values from -6 to 6
- out_grad: bfloat16 [4, 4096, 192], P(('groups', 'design'), ('geom', 'head')), parts along dimension 0, may hold values from -6 to 6
- norm_gain: float32 [192], replicated, may hold values from 0.5 to 1.5
- w_in: bfloat16 [192, 384], replicated, may hold values from -0.4375 to 0.4375
- w_out: bfloat16 [384, 192], replicated, may hold values from -0.3125 to 0.3125
- w_query: bfloat16 [192, 192], replicated, may hold values from -0.4375 to 0.4375
- w_key: bfloat16 [192, 192], replicated, may hold values from -0.4375 to 0.4375
- w_value: bfloat16 [192, 192], replicated, may hold values from -0.4375 to 0.4375
- w_proj: bfloat16 [192, 192], replicated, may hold values from -0.4375 to 0.4375
Outputs:
- attended: bfloat16 [4, 4096, 192], P(('groups', 'design'), ('geom', 'head')), parts along dimension 0
- point_grad: bfloat16 [4, 12288, 192], P(('groups', 'design'), ('geom', 'head')), parts along dimension 0
- grad_in: float32 [384, 384], P('groups'), parts along dimension 0
- grad_out: float32 [768, 192], P('groups'), parts along dimension 0
- grad_query: float32 [384, 192], P('groups'), parts along dimension 0
- grad_key: float32 [384, 192], P('groups'), parts along dimension 0
- grad_value: float32 [384, 192], P('groups'), parts along dimension 0
- grad_proj: float32 [384, 192], P('groups'), parts along dimension 0
- grad_gain: float32 [384], P('groups'), parts along dimension 0
There are 2 independent parts, one for each index of `groups`. A program takes and returns all parts, laid end to end along the dimension named above; an argument that names none is the same for every part. Nothing has to cross between parts.
Inputs may be any that keep to these rules, and one draw needn't show every extreme that they name: `block_anchor`: block index // 12 is the device that holds the block. Each device assigns at most 2 of its blocks to anchors of any one owner (anchor // 16); in every design one owner gets exactly 2 blocks from every device.
All inputs are finite; a program needn't handle non-finite values.
Results may differ from a plain program's by a relative error of at most 0.03.
Values may be sent and summed in bfloat16 or wider, within the bound.
A program may use at most 64 MiB of HBM per device.

v0:
```python
import jax
import jax.numpy as jnp
from jax import lax
from jax.sharding import PartitionSpec as P

HEADS = 3
CAP = 2


def gelu_tanh(values):
    return jax.nn.gelu(values, approximate=True)


def contract_rows(first_arg, second_arg, precision=None):
    return lax.dot_general(
        first_arg,
        second_arg,
        (((0,), (0,)), ((), ())),
        precision=precision,
        preferred_element_type=jnp.float32,
    )


def times_transposed(first_arg, second_arg):
    return lax.dot_general(
        first_arg, second_arg, (((1,), (1,)), ((), ())), preferred_element_type=jnp.float32
    )


def head_split(matrix):
    return matrix.reshape(matrix.shape[0], HEADS, matrix.shape[1] // HEADS)


def on_device(
    point_feats,
    block_anchor,
    anchor_feats,
    query_feats,
    out_grad,
    norm_gain,
    w_in,
    w_out,
    w_query,
    w_key,
    w_value,
    w_proj,
):
    exact_mode = lax.Precision.HIGHEST
    owners = lax.axis_size(("geom", "head"))
    points = point_feats[0]
    assigned = block_anchor[0]
    anchor_rows = anchor_feats[0]
    query_rows = query_feats[0]
    cotangent = out_grad[0]
    blocks = assigned.shape[0]
    feature_width = points.shape[1]
    hidden_width = w_in.shape[1]
    anchors_here = anchor_rows.shape[0]
    block_size = points.shape[0] // blocks
    slot_count = owners * CAP
    target = assigned // anchors_here
    within = assigned - target * anchors_here
    block_order = jnp.arange(blocks)
    earlier = (target[None, :] == target[:, None]) & (block_order[None, :] < block_order[:, None])
    slot_of = target * CAP + jnp.sum(earlier.astype(jnp.int32), axis=1)
    selector = jnp.arange(slot_count)[:, None] == slot_of[None, :]
    select_bf = selector.astype(jnp.bfloat16)
    slot_anchor = jnp.sum(jnp.where(selector, within[None, :] + 1, 0), axis=1) - 1
    pre_act = jnp.dot(points, w_in, preferred_element_type=jnp.float32)
    hidden = gelu_tanh(pre_act).astype(jnp.bfloat16)
    message = jnp.dot(hidden, w_out, preferred_element_type=jnp.float32)
    block_sums = message.reshape(blocks, block_size, feature_width).sum(axis=1)
    outgoing_sums = jnp.dot(selector.astype(jnp.float32), block_sums, precision=exact_mode)
    arrived_sums, arrived_ids = (
        lax.all_to_all(
            outgoing_sums.reshape(owners, CAP, feature_width).astype(jnp.bfloat16),
            ("geom", "head"),
            split_axis=0,
            concat_axis=0,
            tiled=True,
        ).astype(jnp.float32),
        lax.all_to_all(
            slot_anchor.astype(jnp.float32).reshape(owners, CAP).astype(jnp.bfloat16),
            ("geom", "head"),
            split_axis=0,
            concat_axis=0,
            tiled=True,
        ).astype(jnp.float32),
    )
    slot_sums = arrived_sums.reshape(slot_count, feature_width)
    slot_ids = arrived_ids.reshape(slot_count).astype(jnp.int32)
    member = (jnp.arange(anchors_here)[:, None] == slot_ids[None, :]).astype(jnp.float32)
    pooled = jnp.dot(member, slot_sums, precision=exact_mode)
    divisor = jnp.maximum(jnp.sum(member, axis=1) * block_size, 1.0)
    anchor_sum = anchor_rows.astype(jnp.float32) + pooled / divisor[:, None]
    inv_rms = lax.rsqrt(jnp.mean(anchor_sum * anchor_sum, axis=1, keepdims=True) + 1e-06)
    normed = (anchor_sum * inv_rms * norm_gain).astype(jnp.bfloat16)
    key_local = jnp.dot(normed, w_key, preferred_element_type=jnp.float32).astype(jnp.bfloat16)
    value_local = jnp.dot(normed, w_value, preferred_element_type=jnp.float32).astype(jnp.bfloat16)
    all_keys, all_values = (
        lax.all_gather(key_local, ("geom", "head"), axis=0, tiled=True),
        lax.all_gather(value_local, ("geom", "head"), axis=0, tiled=True),
    )
    query_proj = jnp.dot(query_rows, w_query, preferred_element_type=jnp.float32).astype(
        jnp.bfloat16
    )
    score_scale = 1.0 / (feature_width // HEADS) ** 0.5
    query_heads = head_split(query_proj)
    key_heads = head_split(all_keys)
    value_heads = head_split(all_values)
    scores = (
        jnp.einsum("qhd,khd->hqk", query_heads, key_heads, preferred_element_type=jnp.float32)
        * score_scale
    )
    softmax_w = jax.nn.softmax(scores, axis=-1)
    softmax_bf = softmax_w.astype(jnp.bfloat16)
    mixed_heads = (
        jnp.einsum("hqk,khd->qhd", softmax_bf, value_heads, preferred_element_type=jnp.float32)
        .reshape(-1, feature_width)
        .astype(jnp.bfloat16)
    )
    attended = jnp.dot(mixed_heads, w_proj, preferred_element_type=jnp.float32).astype(jnp.bfloat16)
    grad_proj = contract_rows(mixed_heads, cotangent)
    d_mixed = times_transposed(cotangent, w_proj).astype(jnp.bfloat16)
    dmix_heads = head_split(d_mixed)
    d_probs = jnp.einsum(
        "qhd,khd->hqk", dmix_heads, value_heads, preferred_element_type=jnp.float32
    )
    d_scores = (
        softmax_w * (d_probs - jnp.sum(softmax_w * d_probs, axis=-1, keepdims=True)) * score_scale
    ).astype(jnp.bfloat16)
    d_query = (
        jnp.einsum("hqk,khd->qhd", d_scores, key_heads, preferred_element_type=jnp.float32)
        .reshape(-1, feature_width)
        .astype(jnp.bfloat16)
    )
    key_terms = jnp.einsum(
        "hqk,qhd->khd", d_scores, query_heads, preferred_element_type=jnp.float32
    ).reshape(-1, feature_width)
    value_terms = jnp.einsum(
        "hqk,qhd->khd", softmax_bf, dmix_heads, preferred_element_type=jnp.float32
    ).reshape(-1, feature_width)
    grad_query = contract_rows(query_rows, d_query)
    key_sum, value_sum = (
        lax.psum_scatter(
            key_terms.astype(jnp.bfloat16), ("geom", "head"), scatter_dimension=0, tiled=True
        ).astype(jnp.float32),
        lax.psum_scatter(
            value_terms.astype(jnp.bfloat16), ("geom", "head"), scatter_dimension=0, tiled=True
        ).astype(jnp.float32),
    )
    key_grad = key_sum.astype(jnp.bfloat16)
    value_grad = value_sum.astype(jnp.bfloat16)
    grad_key = contract_rows(normed, key_grad)
    grad_value = contract_rows(normed, value_grad)
    d_normed = times_transposed(key_grad, w_key) + times_transposed(value_grad, w_value)
    scaled = d_normed * norm_gain
    grad_gain = jnp.sum(d_normed * anchor_sum * inv_rms, axis=0)
    d_sum = inv_rms * scaled - anchor_sum * inv_rms**3 * jnp.mean(
        scaled * anchor_sum, axis=1, keepdims=True
    )
    d_pooled = d_sum / divisor[:, None]
    slot_grad = contract_rows(member, d_pooled, exact_mode).astype(jnp.bfloat16)
    returned_grad = lax.all_to_all(
        slot_grad.reshape(owners, CAP, feature_width),
        ("geom", "head"),
        split_axis=0,
        concat_axis=0,
        tiled=True,
    )
    block_grad = contract_rows(select_bf, returned_grad.reshape(slot_count, feature_width)).astype(
        jnp.bfloat16
    )
    d_hidden_block = times_transposed(block_grad, w_out)
    d_hidden = jnp.broadcast_to(
        d_hidden_block[:, None, :], (blocks, block_size, hidden_width)
    ).reshape(-1, hidden_width)
    unused_out, gelu_back = jax.vjp(gelu_tanh, pre_act)
    d_pre = gelu_back(d_hidden)[0].astype(jnp.bfloat16)
    hidden_sum = jnp.sum(
        hidden.reshape(blocks, block_size, hidden_width), axis=1, dtype=jnp.float32
    )
    grad_out = contract_rows(hidden_sum, block_grad.astype(jnp.float32), exact_mode)
    grad_in = contract_rows(points, d_pre)
    d_input = times_transposed(d_pre, w_in).astype(jnp.bfloat16)
    reduced = lax.psum(
        (grad_in, grad_out, grad_query, grad_key, grad_value, grad_proj, grad_gain),
        ("geom", "design", "head"),
    )
    return (
        attended[None],
        d_input[None],
        reduced[0],
        reduced[1],
        reduced[2],
        reduced[3],
        reduced[4],
        reduced[5],
        reduced[6],
    )


def solution(mesh):
    placed = (
        P(("groups", "design"), ("geom", "head"), None),
        P(("groups", "design"), ("geom", "head")),
        P(("groups", "design"), ("geom", "head"), None),
        P(("groups", "design"), ("geom", "head"), None),
        P(("groups", "design"), ("geom", "head"), None),
        P(),
        P(),
        P(),
        P(),
        P(),
        P(),
        P(),
    )
    return jax.shard_map(
        on_device,
        mesh=mesh,
        in_specs=placed,
        out_specs=(
            P(("groups", "design"), ("geom", "head"), None),
            P(("groups", "design"), ("geom", "head"), None),
            P("groups", None),
            P("groups", None),
            P("groups", None),
            P("groups", None),
            P("groups", None),
            P("groups", None),
            P("groups"),
        ),
        check_vma=False,
    )
```

profile of v0, /device:TPU:0, one launch (start us, length us, event | category | flops | bytes accessed | tf_op | source)
XLA Modules:
  0.0 259.6 jit_solution(16616870421361154867)
XLA Ops:
  7.2 0.7 and_select_fusion
  7.9 0.7 add_bitcast_fusion
  8.6 0.2 convert_reduce_fusion.2
  8.8 0.1 select_reduce_fusion
  8.9 0.7 convert_element_type.190
  9.6 6.4 %all-to-all-start = ((bf16[8,1,2]{2,1,0:T(2,128)(2,1)}), bf16[8,1,2]{2,1,0:T(2,128)(2,1)S(1)}, u32[]{:S(2)}, u32[]{:S(2)}) async-start(bf16[8,1,2]{2,1,0:T(2,128)(2,1)} %convert_element_type.190), calls=%async_computation | async-start | bytes 8192 | tf_op jit(solution)/shard_map/all_to_all | solution.py:82
  16.0 3.2 %multiply_convert_fusion = (bf16[1536,384]{1,0:T(8,128)(2,1)S(1)}, f32[1536,384]{1,0:T(8,128)}) fusion(bf16[192,384]{1,0:T(8,128)(2,1)} %param.18, bf16[1,1536,192]{1,2,0:T(8,128)(2,1)S(1)} %copy-done), kind=kOutput, calls=%fused_computation.19 | convolution fusion | flops 231800832 | bytes 4276224 | tf_op jit(solution)/shard_map/dot_general | solution.py:69
  19.2 0.8 convert_reduce_fusion
  20.0 0.6 fusion.64
  20.6 0.2 reshape.166
  20.8 0.1 copy-done.1
  20.9 1.2 convolution_convert_fusion.5
  22.1 1.2 convolution_convert_fusion.1
  23.3 0.5 reduce_sum.95
  23.8 0.2 convolution_convert_fusion.12
  23.9 0.7 copy.50
  24.6 5.1 %all-to-all-start.1 = ((bf16[8,2,192]{2,1,0:T(2,128)(2,1)}), bf16[8,2,192]{2,1,0:T(2,128)(2,1)S(1)}, u32[]{:S(2)}, u32[]{:S(2)}) async-start(bf16[8,2,192]{2,1,0:T(2,128)(2,1)} %copy.50), calls=%async_computation.1 | async-start | bytes 16384 | tf_op jit(solution)/shard_map/all_to_all | solution.py:75
  29.8 0.1 convert_element_type.158
  29.9 0.1 convert_reduce_fusion.1
  30.0 5.3 %all-to-all-done.1 = bf16[8,2,192]{2,1,0:T(2,128)(2,1)S(1)} async-done(((bf16[8,2,192]{2,1,0:T(2,128)(2,1)}), bf16[8,2,192]{2,1,0:T(2,128)(2,1)S(1)}, u32[]{:S(2)}, u32[]{:S(2)}) %all-to-all-start.1) | async-done | bytes 6176 | tf_op jit(solution)/shard_map/all_to_all | solution.py:75
  35.4 0.2 multiply_reduce_fusion.3
  35.6 0.1 multiply_convert_fusion.1
  35.7 0.1 convolution_convert_fusion.10
  35.8 0.1 convolution_convert_fusion.11
  36.0 14.0 %all_gather.6 = bf16[128,192]{1,0:T(8,128)(2,1)S(1)} all-gather(bf16[16,192]{1,0:T(8,128)(2,1)S(1)} %convolution_convert_fusion.11), channel_id=1, replica_groups=mesh['groups'=2,'geom'=4,'design'=2,'head'=2] {'geom','head'}, dimensions={0}, use_global_device_ids=true | all-gather | bytes 55296 | tf_op jit(solution)/shard_map/all_gather | solution.py:102
  50.0 0.1 copy.51
  50.1 14.0 %all_gather.7 = bf16[128,192]{1,0:T(8,128)(2,1)S(1)} all-gather(bf16[16,192]{1,0:T(8,128)(2,1)S(1)} %convolution_convert_fusion.10), channel_id=1, replica_groups=mesh['groups'=2,'geom'=4,'design'=2,'head'=2] {'geom','head'}, dimensions={0}, use_global_device_ids=true | all-gather | bytes 55296 | tf_op jit(solution)/shard_map/all_gather | solution.py:101
  64.1 0.1 copy.52
  64.2 0.3 fusion.65
  64.5 1.3 fusion.63
  65.8 1.8 convolution_convert_fusion.7
  67.6 1.8 convolution_convert_fusion.2
  69.4 0.6 convolution_convert_fusion.4
  70.0 0.9 convolution_bitcast_fusion.1
  70.9 0.7 copy.64
  71.7 0.0 reduce-scatter.9.cloned.1.call-start
  71.7 0.9 fusion.30
  72.6 0.6 convolution_convert_fusion.6
  73.2 0.7 copy.66
  74.0 26.5 %reduce-scatter.7.cloned.1.call-done = bf16[16,192]{1,0:T(8,128)(2,1)} async-done(((bf16[128,192]{1,0:T(8,128)(2,1)}), bf16[16,192]{1,0:T(8,128)(2,1)}) %reduce-scatter.7.cloned.1.call-update) | async-done | bytes 6160
  100.5 0.8 fusion.66
  101.4 30.6 %reduce-scatter.9.cloned.1.call-done = bf16[16,192]{1,0:T(8,128)(2,1)} async-done(((bf16[128,192]{1,0:T(8,128)(2,1)}), bf16[16,192]{1,0:T(8,128)(2,1)}) %reduce-scatter.9.cloned.1.call-update) | async-done | bytes 6160
  132.0 1.0 multiply_reduce_fusion.1
  133.0 0.2 convolution_convert_fusion.9
  133.2 0.6 reshape.172
  133.8 3.3 %all-to-all-start.2 = ((bf16[8,2,192]{2,1,0:T(2,128)(2,1)}), bf16[8,2,192]{2,1,0:T(2,128)(2,1)S(1)}, u32[]{:S(2)}, u32[]{:S(2)}) async-start(bf16[8,2,192]{2,1,0:T(2,128)(2,1)} %reshape.172), calls=%async_computation.2 | async-start | bytes 16384 | tf_op jit(solution)/shard_map/all_to_all | solution.py:164
  137.2 1.6 fusion.70
  138.8 1.6 fusion.69
  140.4 2.3 all-to-all-done.2
  142.7 0.2 convolution_convert_fusion.8
  142.9 0.1 fusion.67
  143.0 1.1 fusion.68
  144.1 3.2 %fusion.9 = bf16[1536,384]{1,0:T(8,128)(2,1)S(1)} fusion(f32[1536,384]{1,0:T(8,128)} %get-tuple-element.58, f32[12,384]{1,0:T(8,128)S(1)} %fusion.67), kind=kLoop, calls=%fused_computation.14 | loop fusion | flops 11796480 | bytes 3557376 | tf_op jit(solution)/shard_map/convert_element_type | solution.py:179
  147.4 1.2 convolution_bitcast_fusion
  148.6 0.9 fusion.19
  149.5 32.4 %psum.55 = f32[192]{0:T(256)} all-reduce(f32[192]{0:T(256)S(1)} %get-tuple-element.45), channel_id=1, replica_groups=mesh['groups'=2,'geom'=4,'design'=2,'head'=2] {'geom','design','head'}, use_global_device_ids=true, to_apply=%region_19.20 | all-reduce | flops 192 | bytes 1536 | tf_op jit(solution)/shard_map/psum | solution.py:186
  181.9 1.4 fusion.2
  183.3 60.8 %all-reduce.3.cloned.1.call-done = (f32[192,384]{1,0:T(8,128)}, f32[384,192]{0,1:T(8,128)}, f32[192,192]{0,1:T(8,128)}, f32[192,192]{1,0:T(8,128)}, f32[192,192]{1,0:T(8,128)}, /*index=5*/f32[192,192]{1,0:T(8,128)}) async-done(((f32[192,384]{1,0:T(8,128)}, f32[384,192]{0,1:T(8,128)}, f32[192,192]{0,1:T(8,128)}, f32[192,192]{1,0:T(8,128)}, f32[192,192]{1,0:T(8,128)}, /*index=5*/f32[192,192]{1,0:T(8,128)}), ...) | async-done | bytes 1179664 | tf_op jit(solution)/shard_map/psum | solution.py:186
  244.0 1.8 copy.57
  245.8 1.7 copy.74
  247.5 1.7 copy.75
  249.2 1.6 copy.76
  250.8 1.6 copy.77
  252.4 0.7 copy.78
  (40 shorter events, 0.3 us)
Async XLA Ops:
  7.2 8.8 %copy-start = (bf16[1,1536,192]{1,2,0:T(8,128)(2,1)S(1)}, bf16[1,1536,192]{1,2,0:T(8,128)(2,1)}, u32[]{:S(2)}) copy-start(bf16[1,1536,192]{1,2,0:T(8,128)(2,1)} %param.12) | copy-start | bytes 1769476
  9.6 15.0 %all-to-all-start = ((bf16[8,1,2]{2,1,0:T(2,128)(2,1)}), bf16[8,1,2]{2,1,0:T(2,128)(2,1)S(1)}, u32[]{:S(2)}, u32[]{:S(2)}) async-start(bf16[8,1,2]{2,1,0:T(2,128)(2,1)} %convert_element_type.190), calls=%async_computation | async-start | bytes 8192 | tf_op jit(solution)/shard_map/all_to_all | solution.py:82
  16.0 4.0 %copy-start.3 = (bf16[384,192]{0,1:T(8,128)(2,1)S(1)}, bf16[384,192]{0,1:T(8,128)(2,1)}, u32[]{:S(2)}) copy-start(bf16[384,192]{0,1:T(8,128)(2,1)} %param.19) | copy-start | bytes 442372
  20.0 0.9 copy-start.1
  20.6 15.0 %copy-start.11 = (f32[192]{0:T(256)S(1)}, f32[192]{0:T(256)}, u32[]{:S(2)}) copy-start(f32[192]{0:T(256)} %param.17) | copy-start | bytes 2308
  20.9 14.4 %copy-start.12 = (bf16[1,16,192]{2,1,0:T(8,128)(2,1)S(1)}, bf16[1,16,192]{2,1,0:T(8,128)(2,1)}, u32[]{:S(2)}) copy-start(bf16[1,16,192]{2,1,0:T(8,128)(2,1)} %param.14) | copy-start | bytes 18436
  20.9 14.8 %copy-start.6 = (bf16[192,192]{1,0:T(8,128)(2,1)S(1)}, bf16[192,192]{1,0:T(8,128)(2,1)}, u32[]{:S(2)}) copy-start(bf16[192,192]{1,0:T(8,128)(2,1)} %param.21) | copy-start | bytes 221188
  20.9 14.9 %copy-start.5 = (bf16[192,192]{1,0:T(8,128)(2,1)S(1)}, bf16[192,192]{1,0:T(8,128)(2,1)}, u32[]{:S(2)}) copy-start(bf16[192,192]{1,0:T(8,128)(2,1)} %param.22) | copy-start | bytes 221188
  24.6 10.7 %all-to-all-start.1 = ((bf16[8,2,192]{2,1,0:T(2,128)(2,1)}), bf16[8,2,192]{2,1,0:T(2,128)(2,1)S(1)}, u32[]{:S(2)}, u32[]{:S(2)}) async-start(bf16[8,2,192]{2,1,0:T(2,128)(2,1)} %copy.50), calls=%async_computation.1 | async-start | bytes 16384 | tf_op jit(solution)/shard_map/all_to_all | solution.py:75
  29.7 70.8 %reduce-scatter.7.cloned.1.call-start = ((), (), s32[]{:S(2)}) async-start(), calls=%async_computation.5 | async-start | bytes 73728
  69.4 2.3 copy-start.2
  71.7 60.3 %reduce-scatter.9.cloned.1.call-start = ((), (), s32[]{:S(2)}) async-start(), calls=%async_computation.6 | async-start | bytes 73728
  72.6 70.3 %copy-start.4 = (bf16[384,192]{0,1:T(8,128)(2,1)S(1)}, bf16[384,192]{0,1:T(8,128)(2,1)}, u32[]{:S(2)}) copy-start(bf16[384,192]{0,1:T(8,128)(2,1)} %param.19) | copy-start | bytes 442372
  72.6 70.4 %copy-start.10 = (f32[12,384]{1,0:T(8,128)S(1)}, f32[12,384]{1,0:T(8,128)}, u32[]{:S(2)}) copy-start(f32[12,384]{1,0:T(8,128)} %convert_reduce_fusion) | copy-start | bytes 55300
  133.8 8.9 %all-to-all-start.2 = ((bf16[8,2,192]{2,1,0:T(2,128)(2,1)}), bf16[8,2,192]{2,1,0:T(2,128)(2,1)S(1)}, u32[]{:S(2)}, u32[]{:S(2)}) async-start(bf16[8,2,192]{2,1,0:T(2,128)(2,1)} %reshape.172), calls=%async_computation.2 | async-start | bytes 16384 | tf_op jit(solution)/shard_map/all_to_all | solution.py:164
  137.1 106.9 %all-reduce.3.cloned.1.call-start = ((), (), s32[]{:S(2)}) async-start(), calls=%async_computation.7 | async-start | bytes 2752512 | tf_op jit(solution)/shard_map/psum | solution.py:186
  147.3 1.2 copy-start.7
  147.3 34.6 %copy-start.9 = (bf16[192,384]{1,0:T(8,128)(2,1)S(1)}, bf16[192,384]{1,0:T(8,128)(2,1)}, u32[]{:S(2)}) copy-start(bf16[192,384]{1,0:T(8,128)(2,1)} %param.18) | copy-start | bytes 442372
  244.0 8.4 %copy-start.8 = (f32[192,192]{1,0:T(8,128)S(1)}, f32[192,192]{1,0:T(8,128)}, u32[]{:S(2)}) copy-start(f32[192,192]{1,0:T(8,128)} %get-tuple-element.71) | copy-start | bytes 442372
Sparse Core Ops, SparseCore 0:
  71.8 28.6 reduce-scatter.6
  103.3 28.5 reduce-scatter.8
  148.7 95.3 all-reduce.2
where the time goes:
time: 260 us
  waiting for transfers between devices  126 us (48%)
  blocking collectives  60.4 us (23%)
  matrix products  25.1 us (10%)
  starting transfers between devices  14.9 us (6%)
  between operations  14 us (5%)
  local copies, waits for them, and re-layouts  13.3 us (5%)
  other arithmetic  6.46 us (2%)
    psum x1, waiting for transfers between devices, on_device(): lax.psum((grad_in, grad_out, grad_query, grad_key, grad_value, grad_proj,...  60.8 us
    unnamed x5, waiting for transfers between devices  57.2 us
    psum x1, blocking collectives, on_device(): lax.psum((grad_in, grad_out, grad_query, grad_key, grad_value, grad_proj,...  32.4 us
    all_gather x1, blocking collectives, on_device(): lax.all_gather(key_local, ('geom', 'head'), axis=0, tiled=True)  14 us
    all_gather x1, blocking collectives, on_device(): lax.all_gather(value_local, ('geom', 'head'), axis=0, tiled=True)  14 us
    unnamed x34, local copies, waits for them, and re-layouts  10.7 us
    dot_general x8, matrix products, contract_rows(): lax.dot_general(first_arg, second_arg, (((0,), (0,)), ((), ())), precisio...  7.61 us
    all_to_all x1, starting transfers between devices, on_device(): lax.all_to_all(slot_anchor.astype(jnp.float32).reshape(owners, CAP).astyp...  6.35 us
  transfers between devices with their start and end apart: 6, of which 5 were waited for; matrix products, arithmetic and copies ran while one was open for 7% of the time, Pallas kernels for 0%

commit v1 on v0

v1 whole, which is shorter than its diff:
```python
import functools

import jax
import jax.numpy as jnp
from jax import lax
from jax.experimental import pallas as pl
from jax.experimental.pallas import tpu as pltpu
from jax.sharding import PartitionSpec as P

HEADS = 3
MESH = pl.DeviceIdType.MESH
F32 = jnp.float32
BF = jnp.bfloat16


def dot(a, b):
    return jnp.dot(a, b, preferred_element_type=F32)


def dot_t(a, b):
    return lax.dot_general(a, b, (((1,), (1,)), ((), ())), preferred_element_type=F32)


def dot_rows(a, b):
    return lax.dot_general(a, b, (((0,), (0,)), ((), ())), preferred_element_type=F32)


def two_parts(value):
    high = value.astype(BF)
    low = (value - high.astype(F32)).astype(BF)
    return high, low


def each(count, body):
    if count <= 8:
        for step in range(1, count):
            body(step)
    else:
        def run(step, carry):
            body(step)
            return carry
        lax.fori_loop(1, count, run, 0)


class Exchange:
    def __init__(self, rank, size, place, send_sem, recv_sem):
        self.rank, self.size, self.place = rank, size, place
        self.send_sem, self.recv_sem = send_sem, recv_sem

    def copy(self, step, src, dst):
        to = lax.rem(self.rank + step, self.size)
        return pltpu.make_async_remote_copy(
            src_ref=src(to),
            dst_ref=dst(self.rank),
            send_sem=self.send_sem.at[to],
            recv_sem=self.recv_sem.at[self.rank],
            device_id=self.place(to),
            device_id_type=MESH,
        )

    def start(self, src, dst):
        self.src, self.dst = src, dst
        each(self.size, lambda step: self.copy(step, src, dst).start())

    def wait_recv(self):
        def one(step):
            peer = lax.rem(self.rank + step, self.size)
            pltpu.make_async_remote_copy(
                src_ref=self.src(peer),
                dst_ref=self.dst(peer),
                send_sem=self.send_sem.at[peer],
                recv_sem=self.recv_sem.at[peer],
                device_id=self.place(peer),
                device_id_type=MESH,
            ).wait_recv()
        each(self.size, one)

    def wait_send(self):
        each(self.size, lambda step: self.copy(step, self.src, self.dst).wait_send())


class Reduce:
    def __init__(self, bufs, quad, line):
        self.parts, self.got, self.lined, self.final = bufs[:4]
        sems = bufs[4]
        self.q, self.z = quad[0], line[0]
        self.one = Exchange(*quad, sems[0], sems[1])
        self.two = Exchange(*line, sems[2], sems[3])
        self.three = Exchange(*quad, sems[4], sems[5])

    def phase1(self):
        self.got[self.q] = self.parts[self.q]
        self.one.start(lambda to: self.parts.at[to], lambda me: self.got.at[me])

    def phase2(self):
        self.one.wait_recv()
        self.lined[self.z] = jnp.sum(self.got[...].astype(F32), axis=0).astype(BF)
        z = self.z
        self.two.start(lambda to: self.lined.at[z], lambda me: self.lined.at[me])

    def phase3(self):
        self.two.wait_recv()
        self.final[self.q] = jnp.sum(self.lined[...].astype(F32), axis=0).astype(BF)
        q = self.q
        self.three.start(lambda to: self.final.at[q], lambda me: self.final.at[me])

    def finish(self):
        self.three.wait_recv()

    def drain(self):
        self.one.wait_send()
        self.two.wait_send()
        self.three.wait_send()


def kernel(
    sizes,
    pts, ids, anc, qry, cot, gain, w_in, w_out, w_query, w_key, w_value, w_proj,
    attended, point_grad, grad_in, grad_out, grad_query, grad_key, grad_value, grad_proj, grad_gain,
    hs, gp, gmat, w_pad, msg, qp, dm, pm, ds, ks, vs, asum, divs, snd2, rcv2, dpool, dhs,
    r1a, r1b, r1c, r1d, r2a, r2b, r2c, r2d, r3a, r3b, r3c, r3d, r4a, r4b, r4c, r4d,
    sem_o, sem_q, sem_z,
):
    n_z, n_x, n_c = sizes
    owners, quads = n_z * n_c, n_x * n_c
    z, x, c = lax.axis_index("geom"), lax.axis_index("design"), lax.axis_index("head")
    me = z * n_c + c
    q = x * n_c + c
    width = w_in.shape[0]
    hidden = w_in.shape[1]
    blocks = ids.shape[1]
    a_here = anc.shape[1]
    rows_b = pts.shape[1] // blocks
    slots = msg.shape[1] - a_here
    anchors = owners * a_here
    queries = qry.shape[1]
    lanes = msg.shape[2]

    def design_place(to):
        return {"geom": lax.div(to, n_c), "head": lax.rem(to, n_c)}

    def quad_place(to):
        return {"design": lax.div(to, n_c), "head": lax.rem(to, n_c)}

    def line_place(to):
        return {"geom": to}

    quad = (q, quads, quad_place)
    line = (z, n_z, line_place)
    exch = [
        Exchange(me, owners, design_place, sem_o.at[2 * i], sem_o.at[2 * i + 1]) for i in range(3)
    ]

    def reducer(i, bufs):
        sems = [sem_q.at[4 * i], sem_q.at[4 * i + 1], sem_z.at[2 * i], sem_z.at[2 * i + 1],
                sem_q.at[4 * i + 2], sem_q.at[4 * i + 3]]
        return Reduce((*bufs, sems), quad, line)

    red_pq = reducer(0, (r1a, r1b, r1c, r1d))
    red_kv = reducer(1, (r2a, r2b, r2c, r2d))
    red_in = reducer(2, (r3a, r3b, r3c, r3d))
    red_out = reducer(3, (r4a, r4b, r4c, r4d))

    barrier = pltpu.get_barrier_semaphore()

    def greet(step):
        to = lax.rem(me + step, owners)
        pl.semaphore_signal(barrier, inc=1, device_id=design_place(to), device_id_type=MESH)

    each(owners, greet)

    def greet_across(step):
        other = lax.rem(x + step, n_x)
        for core in range(n_c):
            pl.semaphore_signal(
                barrier, inc=1, device_id={"design": other, "head": core}, device_id_type=MESH
            )

    each(n_x, greet_across)

    hs[...] = jnp.zeros_like(hs)
    c0 = 0.7978845608028654
    c1 = 0.044715 * c0

    def one_block(b, carry):
        rows = pl.ds(pl.multiple_of(b * rows_b, rows_b), rows_b)
        pre = dot(pts[0, rows, :], w_in[...])
        sq = pre * pre
        t = jnp.tanh(pre * (c0 + c1 * sq))
        half = 0.5 + 0.5 * t
        hid = (pre * half).astype(BF)
        hs[pl.ds(b, 1), :] = jnp.sum(hid.astype(F32), axis=0, keepdims=True)
        slope = half + 0.5 * pre * (1.0 - t * t) * (c0 + (3.0 * c1) * sq)
        gp[b] = slope.astype(BF)
        return carry

    lax.fori_loop(0, blocks, one_block, 0)

    w_pad[...] = jnp.zeros_like(w_pad)
    w_pad[:, 0:width] = w_out[...]
    hs_high, hs_low = two_parts(hs[...])
    sums = dot(hs_high, w_pad[...]) + dot(hs_low, w_pad[...])
    row = lax.broadcasted_iota(jnp.int32, (slots, lanes), 0)
    lane = lax.broadcasted_iota(jnp.int32, (slots, lanes), 1)
    own_o = jnp.full((slots, lanes), -1, jnp.int32)
    own_w = jnp.zeros((slots, lanes), jnp.int32)
    for i in range(blocks):
        number = ids[0, i]
        block_owner = lax.div(number, a_here)
        own_o = jnp.where(row == i, block_owner, own_o)
        own_w = jnp.where(row == i, number - block_owner * a_here, own_w)
    own_o = own_o.astype(F32)
    own_w = own_w.astype(F32)
    sums = jnp.where(lane == width, own_o, sums)
    sums = jnp.where(lane == width + 1, own_w, sums)
    sums = jnp.where(lane == width + 2, 1.0, sums)
    msg[me, 0:slots, :] = sums.astype(BF)
    msg[me, slots:, :] = jnp.zeros((a_here, lanes), BF)
    msg[me, slots:, 0:width] = anc[0]

    pl.semaphore_wait(barrier, owners - 1 + (n_x - 1) * n_c)
    exch[0].start(lambda to: msg.at[me], lambda rank: msg.at[rank])

    qp[...] = dot(qry[0], w_query[...]).astype(BF)
    dm[...] = dot_t(cot[0], w_proj[...]).astype(BF)

    def one_product(b, carry):
        rows = pl.ds(pl.multiple_of(b * rows_b, rows_b), rows_b)
        gmat[b] = dot_rows(pts[0, rows, :], gp[b])
        return carry

    lax.fori_loop(0, blocks, one_product, 0)

    exch[0].wait_recv()
    arrived = msg[:, 0:slots, :].reshape(owners * slots, lanes)
    wide = arrived.astype(F32)
    numbers = wide[:, width:width + 1] * float(a_here) + wide[:, width + 1:width + 2]
    anchor_lane = lax.broadcasted_iota(jnp.int32, (owners * slots, anchors), 1).astype(F32)
    member = jnp.where(numbers == anchor_lane, 1.0, 0.0).astype(BF)
    pooled = dot_rows(member, arrived)
    divisor = jnp.maximum(pooled[:, width + 2:width + 3] * float(rows_b), 1.0)
    anchor_rows = msg[:, slots:, 0:width].reshape(anchors, width).astype(F32)
    anchor_sum = anchor_rows + pooled[:, 0:width] / divisor
    asum[...] = anchor_sum
    divs[...] = jnp.broadcast_to(divisor, divs.shape)
    gain_row = gain[...]
    inv_rms = lax.rsqrt(jnp.mean(anchor_sum * anchor_sum, axis=1, keepdims=True) + 1e-06)
    normed = (anchor_sum * inv_rms * gain_row).astype(BF)
    keys = dot(normed, w_key[...]).astype(BF)
    values = dot(normed, w_value[...]).astype(BF)
    depth = width // HEADS
    head_lane = lax.broadcasted_iota(jnp.int32, (anchors, width), 1)
    masks = [(head_lane >= h * depth) & (head_lane < (h + 1) * depth) for h in range(HEADS)]
    nothing = jnp.zeros((anchors, width), F32)
    for h in range(HEADS):
        part = slice(h * anchors, (h + 1) * anchors)
        ks[part, :] = jnp.where(masks[h], keys.astype(F32), nothing).astype(BF)
        vs[part, :] = jnp.where(masks[h], values.astype(F32), nothing).astype(BF)

    tile = 128
    scale = 1.0 / depth**0.5

    def one_tile(i, carry):
        rows = pl.ds(pl.multiple_of(i * tile, tile), tile)
        scores = dot_t(qp[rows, :], ks[...])
        d_probs = dot_t(dm[rows, :], vs[...])
        for h in range(HEADS):
            part = slice(h * anchors, (h + 1) * anchors)
            s = scores[:, part] * scale
            e = jnp.exp(s - jnp.max(s, axis=1, keepdims=True))
            p = e / jnp.sum(e, axis=1, keepdims=True)
            dp = d_probs[:, part]
            d = p * (dp - jnp.sum(p * dp, axis=1, keepdims=True)) * scale
            pm[rows, part] = p.astype(BF)
            ds[rows, part] = d.astype(BF)
        return carry

    lax.fori_loop(0, queries // tile, one_tile, 0)

    def own_heads(stacked):
        total = jnp.zeros((anchors, width), F32)
        for h in range(HEADS):
            total = jnp.where(masks[h], stacked[h * anchors:(h + 1) * anchors, :], total)
        return total.astype(BF).reshape(owners, a_here, width)

    snd2[:, 0] = own_heads(dot_rows(ds[...], qp[...]))
    snd2[:, 1] = own_heads(dot_rows(pm[...], dm[...]))
    rcv2[me] = snd2[me]
    exch[1].start(lambda to: snd2.at[to], lambda rank: rcv2.at[rank])

    mixed = dot(pm[...], vs[...]).astype(BF)
    attended[0] = dot(mixed, w_proj[...]).astype(BF)
    half_q = quads // 2

    def fill(ref, first, second, rows):
        for j in range(quads):
            src = first if j < half_q else second
            k = j if j < half_q else j - half_q
            ref[j, 0:rows, :] = src[k * rows:(k + 1) * rows, :].astype(BF)

    chunk = 2 * width // quads
    d_query = dot(ds[...], ks[...]).astype(BF)
    fill(r1a, dot_rows(mixed, cot[0]), dot_rows(qry[0], d_query), chunk)
    red_pq.phase1()

    exch[1].wait_recv()
    sum2 = jnp.sum(rcv2[...].astype(F32), axis=0).astype(BF)
    key_grad, value_grad = sum2[0], sum2[1]
    mine = pl.ds(pl.multiple_of(me * a_here, a_here), a_here)
    a_sum = asum[mine, :]
    div_own = divs[mine, 0:1]
    inv = lax.rsqrt(jnp.mean(a_sum * a_sum, axis=1, keepdims=True) + 1e-06)
    d_normed = dot_t(key_grad, w_key[...]) + dot_t(value_grad, w_value[...])
    scaled = d_normed * gain_row
    d_sum = inv * scaled - a_sum * (inv * inv * inv) * jnp.mean(
        scaled * a_sum, axis=1, keepdims=True
    )
    dpool[me] = (d_sum / div_own).astype(BF)
    exch[2].start(lambda to: dpool.at[me], lambda rank: dpool.at[rank])

    gain_part = jnp.sum(d_normed * a_sum * inv, axis=0, keepdims=True)
    own_normed = (a_sum * inv * gain_row).astype(BF)
    fill(r2a, dot_rows(own_normed, key_grad), dot_rows(own_normed, value_grad), chunk)
    extra = jnp.broadcast_to(gain_part, (r2a.shape[1] - chunk, width)).astype(BF)
    for j in range(quads):
        r2a[j, chunk:, :] = extra
    red_kv.phase1()
    red_pq.phase2()

    exch[2].wait_recv()
    own_lane = lax.broadcasted_iota(jnp.int32, (slots, anchors), 1).astype(F32)
    own_number = own_o[:, 0:1] * float(a_here) + own_w[:, 0:1]
    own_member = jnp.where(own_number == own_lane, 1.0, 0.0).astype(BF)
    block_grad = dot(own_member, dpool[...].reshape(anchors, width)).astype(BF)
    dhs[...] = dot_t(block_grad, w_out[...])
    chunk_in = width // quads
    for j in range(quads):
        rows = slice(j * chunk_in, (j + 1) * chunk_in)
        total = jnp.zeros((chunk_in, hidden), F32)
        for b in range(blocks):
            total = total + gmat[b, rows, :] * dhs[b:b + 1, :]
        r3a[j] = total.astype(BF)
    red_in.phase1()
    out_part = dot_rows(hs_high, block_grad) + dot_rows(hs_low, block_grad)
    for j in range(quads):
        r4a[j] = out_part[j * chunk:(j + 1) * chunk, :].astype(BF)
    red_out.phase1()

    def one_back(b, carry):
        rows = pl.ds(pl.multiple_of(b * rows_b, rows_b), rows_b)
        d_pre = (gp[b].astype(F32) * dhs[pl.ds(b, 1), :]).astype(BF)
        point_grad[0, rows, :] = dot_t(d_pre, w_in[...]).astype(BF)
        return carry

    red_kv.phase2()
    lax.fori_loop(0, blocks // 2, one_back, 0)
    red_in.phase2()
    red_out.phase2()
    red_pq.phase3()
    lax.fori_loop(blocks // 2, blocks, one_back, 0)
    red_kv.phase3()
    red_in.phase3()
    red_out.phase3()

    red_pq.finish()
    for j in range(quads):
        ref = grad_proj if j < half_q else grad_query
        k = j if j < half_q else j - half_q
        ref[k * chunk:(k + 1) * chunk, :] = r1d[j].astype(F32)
    red_kv.finish()
    for j in range(quads):
        ref = grad_key if j < half_q else grad_value
        k = j if j < half_q else j - half_q
        ref[k * chunk:(k + 1) * chunk, :] = r2d[j, 0:chunk, :].astype(F32)
    grad_gain[...] = r2d[0, chunk:, :].astype(F32)[0:1, :]
    red_in.finish()
    for j in range(quads):
        grad_in[j * chunk_in:(j + 1) * chunk_in, :] = r3d[j].astype(F32)
    red_out.finish()
    for j in range(quads):
        grad_out[j * chunk:(j + 1) * chunk, :] = r4d[j].astype(F32)

    for item in exch:
        item.wait_send()
    for item in (red_pq, red_kv, red_in, red_out):
        item.drain()


def on_device(sizes, *args):
    points, assigned, anchors, queries, cotangent, gain, w_in, w_out, *squares = args
    n_z, n_x, n_c = sizes
    owners, quads = n_z * n_c, n_x * n_c
    width, hidden = w_in.shape
    blocks = assigned.shape[1]
    a_here = anchors.shape[1]
    rows_b = points.shape[1] // blocks
    slots = -(-blocks // 16) * 16
    lanes = -(-(width + 3) // 128) * 128
    n_q = queries.shape[1]
    total = owners * a_here
    chunk = 2 * width // quads
    chunk_in = width // quads

    def red(rows, cols):
        one = pltpu.VMEM((quads, rows, cols), BF)
        return [one, one, pltpu.VMEM((n_z, rows, cols), BF), one]

    vmem = pl.BlockSpec(memory_space=pltpu.VMEM)
    smem = pl.BlockSpec(memory_space=pltpu.SMEM)
    outs = pl.pallas_call(
        functools.partial(kernel, sizes),
        out_shape=[
            jax.ShapeDtypeStruct(queries.shape, BF),
            jax.ShapeDtypeStruct(points.shape, BF),
            jax.ShapeDtypeStruct((width, hidden), F32),
            jax.ShapeDtypeStruct((hidden, width), F32),
            *[jax.ShapeDtypeStruct((width, width), F32)] * 4,
            jax.ShapeDtypeStruct((1, width), F32),
        ],
        in_specs=[vmem, smem] + [vmem] * 10,
        out_specs=[vmem] * 9,
        scratch_shapes=[
            pltpu.VMEM((slots, hidden), F32),
            pltpu.VMEM((blocks, rows_b, hidden), BF),
            pltpu.VMEM((blocks, width, hidden), F32),
            pltpu.VMEM((hidden, lanes), BF),
            pltpu.VMEM((owners, slots + a_here, lanes), BF),
            pltpu.VMEM((n_q, width), BF),
            pltpu.VMEM((n_q, width), BF),
            pltpu.VMEM((n_q, HEADS * total), BF),
            pltpu.VMEM((n_q, HEADS * total), BF),
            pltpu.VMEM((HEADS * total, width), BF),
            pltpu.VMEM((HEADS * total, width), BF),
            pltpu.VMEM((total, width), F32),
            pltpu.VMEM((total, 128), F32),
            pltpu.VMEM((owners, 2, a_here, width), BF),
            pltpu.VMEM((owners, 2, a_here, width), BF),
            pltpu.VMEM((owners, a_here, width), BF),
            pltpu.VMEM((slots, hidden), F32),
            *red(chunk, width),
            *red(chunk + 16, width),
            *red(chunk_in, hidden),
            *red(chunk, width),
            pltpu.SemaphoreType.DMA((6, owners)),
            pltpu.SemaphoreType.DMA((16, quads)),
            pltpu.SemaphoreType.DMA((8, n_z)),
        ],
        compiler_params=pltpu.CompilerParams(
            collective_id=0, has_side_effects=True, vmem_limit_bytes=56 * 1024 * 1024
        ),
        name="layer",
    )(points, assigned, anchors, queries, cotangent, gain.reshape(1, width), w_in, w_out, *squares)
    return (*outs[:8], outs[8].reshape(width))


def solution(mesh):
    sizes = (mesh.shape["geom"], mesh.shape["design"], mesh.shape["head"])
    rows = P(("groups", "design"), ("geom", "head"), None)
    whole = P("groups", None)
    return jax.shard_map(
        functools.partial(on_device, sizes),
        mesh=mesh,
        in_specs=(rows, P(("groups", "design"), ("geom", "head")), rows, rows, rows, *[P()] * 7),
        out_specs=(rows, rows, *[whole] * 6, P("groups")),
        check_vma=False,
    )
```

time: 260 us -> 62.7 us (0.24)
  waiting for transfers between devices: 126 us -> 0 us
  blocking collectives: 60.4 us -> 0 us
  Pallas kernels: 0 us -> 46.1 us
  matrix products: 25.1 us -> 0 us
  starting transfers between devices: 14.9 us -> 0 us
  between operations: 14 us -> 0.69 us
  other arithmetic: 6.46 us -> 0 us
    psum x1 -> x0, waiting for transfers between devices: 60.8 us -> none  [on_device(): lax.psum((grad_in, grad_out, grad_query, grad_key, grad_value, grad_proj,...]
    unnamed x5 -> x0, waiting for transfers between devices: 57.2 us -> none
    pallas_call x0 -> x1, Pallas kernels: none -> 46.1 us  [on_device(): pl.pallas_call(functools.partial(kernel, sizes), out_shape=[jax.ShapeDtyp...]
    psum x1 -> x0, blocking collectives: 32.4 us -> none  [on_device(): lax.psum((grad_in, grad_out, grad_query, grad_key, grad_value, grad_proj,...]
    all_gather x2 -> x0, blocking collectives: 28 us -> none  [the longest x1 14 us: on_device(): lax.all_gather(key_local, ('geom', 'head'), axis=0, tiled=True)]
    dot_general x26 -> x0, matrix products: 23.7 us -> none  [the longest x8 7.61 us: contract_rows(): lax.dot_general(first_arg, second_arg, (((0,), (0,)), ((), ())), precisio...]
    all_to_all x3 -> x0, starting transfers between devices: 14.8 us -> none  [the longest x1 6.35 us: on_device(): lax.all_to_all(slot_anchor.astype(jnp.float32).reshape(owners, CAP).astyp...]
    all_to_all x3 -> x0, waiting for transfers between devices: 7.66 us -> none  [the longest x1 5.33 us: on_device(): lax.all_to_all(outgoing_sums.reshape(owners, CAP, feature_width).astype(j...]
  transfers between devices with their start and end apart: 6 -> 0, of which waited for: 5 -> 0; matrix products, arithmetic and copies ran while one was open for 7% -> 0% of each run, Pallas kernels for 0% -> 0%
where the time goes in v1:
time: 62.7 us; the launch traced here: 62.3 us
  Pallas kernels  46.1 us (74%)
  local copies, waits for them, and re-layouts  15.6 us (25%)
  between operations  0.69 us (1%)
    pallas_call x1, Pallas kernels, on_device(): pl.pallas_call(functools.partial(kernel, sizes), out_shape=[jax.ShapeDtyp...  46.1 us
    unnamed x31, local copies, waits for them, and re-layouts  15.6 us

profile of v1, /device:TPU:0, one launch (start us, length us, event | category | flops | bytes accessed | tf_op | source)
XLA Modules:
  0.0 62.3 jit_solution(1756593235292884824)
XLA Ops:
  0.6 0.0 copy-start.3
  0.7 0.0 copy-start.1
  0.7 1.8 %copy.24.w_out = bf16[384,192]{1,0:T(8,128)(2,1)} copy(bf16[384,192]{0,1:T(8,128)(2,1)} %param.19) | data formatting | bytes 294912 | tf_op args[7]
  2.5 0.0 copy-done.3
  2.5 0.8 %copy.22.qry = bf16[1,512,192]{2,1,0:T(8,128)(2,1)} copy(bf16[1,512,192]{1,2,0:T(8,128)(2,1)S(1)} %copy-done.3) | data formatting | bytes 393216 | tf_op args[3]
  3.3 1.8 %copy.23.cot = bf16[1,512,192]{2,1,0:T(8,128)(2,1)} copy(bf16[1,512,192]{1,2,0:T(8,128)(2,1)} %param.16) | data formatting | bytes 393216 | tf_op args[4]
  5.1 0.0 copy-done.1
  5.1 1.2 %copy.21.pts = bf16[1,1536,192]{2,1,0:T(8,128)(2,1)} copy(bf16[1,1536,192]{1,2,0:T(8,128)(2,1)S(1)} %copy-done.1) | data formatting | bytes 1179648 | tf_op args[0]
  6.2 46.1 %layer.1 = (bf16[1,512,192]{2,1,0:T(8,128)(2,1)}, bf16[1,1536,192]{2,1,0:T(8,128)(2,1)}, f32[192,384]{1,0:T(8,128)}, f32[384,192]{1,0:T(8,128)}, f32[192,192]{1,...) custom-call(bf16[1,1536,192]{2,1,0:T(8,128)(2,1)} %copy.21.pts, ...), custom_call_target="tpu_custom_call" | custom-call | tf_op jit(solution)/shard_map/layer/pallas_call | solution.py:410
  52.3 0.0 copy-start
  52.3 1.8 %copy.25 = bf16[1,512,192]{1,2,0:T(8,128)(2,1)} copy(bf16[1,512,192]{2,1,0:T(8,128)(2,1)} %get-tuple-element.27) | data formatting | bytes 393216
  54.1 1.9 %copy.27 = f32[384,192]{0,1:T(8,128)} copy(f32[384,192]{1,0:T(8,128)} %get-tuple-element.30) | data formatting | bytes 589824
  56.0 0.0 copy-done
  56.0 0.0 copy-start.2
  56.0 1.1 %copy.26 = bf16[1,1536,192]{1,2,0:T(8,128)(2,1)} copy(bf16[1,1536,192]{2,1,0:T(8,128)(2,1)S(1)} %copy-done) | data formatting | bytes 1179648
  57.1 0.0 copy-done.2
  57.1 0.0 copy-start.7
  57.1 0.7 %copy.34 = f32[192,384]{1,0:T(8,128)} copy(f32[192,384]{1,0:T(8,128)S(1)} %copy-done.2) | data formatting | bytes 589824
  57.8 0.3 copy-done.7
  58.1 0.0 copy-start.6
  58.1 0.7 %copy.35 = f32[192,192]{1,0:T(8,128)} copy(f32[192,192]{1,0:T(8,128)S(1)} %copy-done.7) | data formatting | bytes 294912
  58.8 0.3 copy-done.6
  59.1 0.0 copy-start.5
  59.1 0.7 %copy.36 = f32[192,192]{1,0:T(8,128)} copy(f32[192,192]{1,0:T(8,128)S(1)} %copy-done.6) | data formatting | bytes 294912
  59.8 0.3 copy-done.5
  60.1 0.0 copy-start.4
  60.1 0.7 %copy.37 = f32[192,192]{1,0:T(8,128)} copy(f32[192,192]{1,0:T(8,128)S(1)} %copy-done.5) | data formatting | bytes 294912
  60.8 0.3 copy-done.4
  61.1 0.0 copy-start.8
  61.1 0.7 %copy.38 = f32[192,192]{1,0:T(8,128)} copy(f32[192,192]{1,0:T(8,128)S(1)} %copy-done.4) | data formatting | bytes 294912
  61.8 0.0 copy-done.8
  61.8 0.6 copy.39
Async XLA Ops:
  0.6 1.8 %copy-start.3 = (bf16[1,512,192]{1,2,0:T(8,128)(2,1)S(1)}, bf16[1,512,192]{1,2,0:T(8,128)(2,1)}, u32[]{:S(2)}) copy-start(bf16[1,512,192]{1,2,0:T(8,128)(2,1)} %param.15) | copy-start | bytes 589828
  0.7 4.4 %copy-start.1 = (bf16[1,1536,192]{1,2,0:T(8,128)(2,1)S(1)}, bf16[1,1536,192]{1,2,0:T(8,128)(2,1)}, u32[]{:S(2)}) copy-start(bf16[1,1536,192]{1,2,0:T(8,128)(2,1)} %param.12) | copy-start | bytes 1769476
  52.3 3.7 %copy-start = (bf16[1,1536,192]{2,1,0:T(8,128)(2,1)S(1)}, bf16[1,1536,192]{2,1,0:T(8,128)(2,1)}, u32[]{:S(2)}) copy-start(bf16[1,1536,192]{2,1,0:T(8,128)(2,1)} %get-tuple-element.28) | copy-start | bytes 1769476
  56.0 1.1 %copy-start.2 = (f32[192,384]{1,0:T(8,128)S(1)}, f32[192,384]{1,0:T(8,128)}, u32[]{:S(2)}) copy-start(f32[192,384]{1,0:T(8,128)} %get-tuple-element.47) | copy-start | bytes 884740
  57.1 1.0 %copy-start.7 = (f32[192,192]{1,0:T(8,128)S(1)}, f32[192,192]{1,0:T(8,128)}, u32[]{:S(2)}) copy-start(f32[192,192]{1,0:T(8,128)} %get-tuple-element.49) | copy-start | bytes 442372
  58.1 1.0 %copy-start.6 = (f32[192,192]{1,0:T(8,128)S(1)}, f32[192,192]{1,0:T(8,128)}, u32[]{:S(2)}) copy-start(f32[192,192]{1,0:T(8,128)} %get-tuple-element.50) | copy-start | bytes 442372
  59.1 1.0 %copy-start.5 = (f32[192,192]{1,0:T(8,128)S(1)}, f32[192,192]{1,0:T(8,128)}, u32[]{:S(2)}) copy-start(f32[192,192]{1,0:T(8,128)} %get-tuple-element.51) | copy-start | bytes 442372
  60.1 1.0 %copy-start.4 = (f32[192,192]{1,0:T(8,128)S(1)}, f32[192,192]{1,0:T(8,128)}, u32[]{:S(2)}) copy-start(f32[192,192]{1,0:T(8,128)} %get-tuple-element.52) | copy-start | bytes 442372
  61.1 0.7 %copy-start.8 = (f32[1,192]{1,0:T(1,128)S(1)}, f32[1,192]{1,0:T(1,128)}, u32[]{:S(2)}) copy-start(f32[1,192]{1,0:T(1,128)} %get-tuple-element.26) | copy-start | bytes 2308

commit v2 on v1

--- a/solution.py
+++ b/solution.py
@@ -116,9 +116,9 @@
 def kernel(
     sizes,
     pts, ids, anc, qry, cot, gain, w_in, w_out, w_query, w_key, w_value, w_proj,
-    attended, point_grad, grad_in, grad_out, grad_query, grad_key, grad_value, grad_proj, grad_gain,
-    hs, gp, gmat, w_pad, msg, qp, dm, pm, ds, ks, vs, asum, divs, snd2, rcv2, dpool, dhs,
-    r1a, r1b, r1c, r1d, r2a, r2b, r2c, r2d, r3a, r3b, r3c, r3d, r4a, r4b, r4c, r4d,
+    attended, point_grad, fin_in, fin_pq, fin_kv,
+    hs, gp, gmat, w_turned, w_pad, msg, qp, dm, pm, ds, ks, vs, asum, divs, snd2, rcv2, dpool,
+    r1a, r1b, r1c, r1d, r2a, r2b, r2c, r2d, r3a, r3b, r3c, r3d,
     sem_o, sem_q, sem_z,
 ):
     n_z, n_x, n_c = sizes
@@ -130,10 +130,10 @@
     hidden = w_in.shape[1]
     blocks = ids.shape[1]
     a_here = anc.shape[1]
-    rows_b = pts.shape[1] // blocks
+    rows_b = pts.shape[2] // blocks
     slots = msg.shape[1] - a_here
     anchors = owners * a_here
-    queries = qry.shape[1]
+    queries = qry.shape[2]
     lanes = msg.shape[2]
 
     def design_place(to):
@@ -159,7 +159,6 @@
     red_pq = reducer(0, (r1a, r1b, r1c, r1d))
     red_kv = reducer(1, (r2a, r2b, r2c, r2d))
     red_in = reducer(2, (r3a, r3b, r3c, r3d))
-    red_out = reducer(3, (r4a, r4b, r4c, r4d))
 
     barrier = pltpu.get_barrier_semaphore()
 
@@ -178,28 +177,31 @@
 
     each(n_x, greet_across)
 
-    hs[...] = jnp.zeros_like(hs)
     c0 = 0.7978845608028654
     c1 = 0.044715 * c0
-
-    def one_block(b, carry):
-        rows = pl.ds(pl.multiple_of(b * rows_b, rows_b), rows_b)
-        pre = dot(pts[0, rows, :], w_in[...])
+    w_turned[...] = w_in[...].T
+    wide_b = 2 if blocks % 2 == 0 else 1
+    span = wide_b * rows_b
+    span_row = lax.broadcasted_iota(jnp.int32, (slots, span), 0)
+    span_block = lax.broadcasted_iota(jnp.int32, (slots, span), 1) // rows_b
+    hidden_sum = jnp.zeros((slots, hidden), F32)
+    for i in range(blocks // wide_b):
+        cols = slice(i * span, (i + 1) * span)
+        pre = dot(w_turned[...], pts[0, :, cols])
         sq = pre * pre
         t = jnp.tanh(pre * (c0 + c1 * sq))
         half = 0.5 + 0.5 * t
         hid = (pre * half).astype(BF)
-        hs[pl.ds(b, 1), :] = jnp.sum(hid.astype(F32), axis=0, keepdims=True)
+        pick = jnp.where(span_row == span_block + i * wide_b, 1.0, 0.0).astype(BF)
+        hidden_sum = hidden_sum + dot_t(pick, hid)
         slope = half + 0.5 * pre * (1.0 - t * t) * (c0 + (3.0 * c1) * sq)
-        gp[b] = slope.astype(BF)
-        return carry
-
-    lax.fori_loop(0, blocks, one_block, 0)
+        gp[:, cols] = slope.astype(BF)
+    hs[...] = hidden_sum
 
     w_pad[...] = jnp.zeros_like(w_pad)
-    w_pad[:, 0:width] = w_out[...]
-    hs_high, hs_low = two_parts(hs[...])
-    sums = dot(hs_high, w_pad[...]) + dot(hs_low, w_pad[...])
+    w_pad[0:width, :] = w_out[...]
+    hs_high, hs_low = two_parts(hidden_sum)
+    sums = dot_t(hs_high, w_pad[...]) + dot_t(hs_low, w_pad[...])
     row = lax.broadcasted_iota(jnp.int32, (slots, lanes), 0)
     lane = lax.broadcasted_iota(jnp.int32, (slots, lanes), 1)
     own_o = jnp.full((slots, lanes), -1, jnp.int32)
@@ -221,15 +223,11 @@
     pl.semaphore_wait(barrier, owners - 1 + (n_x - 1) * n_c)
     exch[0].start(lambda to: msg.at[me], lambda rank: msg.at[rank])
 
-    qp[...] = dot(qry[0], w_query[...]).astype(BF)
-    dm[...] = dot_t(cot[0], w_proj[...]).astype(BF)
-
-    def one_product(b, carry):
-        rows = pl.ds(pl.multiple_of(b * rows_b, rows_b), rows_b)
-        gmat[b] = dot_rows(pts[0, rows, :], gp[b])
-        return carry
-
-    lax.fori_loop(0, blocks, one_product, 0)
+    qp[...] = dot_rows(w_query[...], qry[0]).astype(BF)
+    dm[...] = dot(w_proj[...], cot[0]).astype(BF)
+    for b in range(blocks):
+        cols = slice(b * rows_b, (b + 1) * rows_b)
+        gmat[b] = dot_t(pts[0, :, cols], gp[:, cols])
 
     exch[0].wait_recv()
     arrived = msg[:, 0:slots, :].reshape(owners * slots, lanes)
@@ -257,25 +255,21 @@
         ks[part, :] = jnp.where(masks[h], keys.astype(F32), nothing).astype(BF)
         vs[part, :] = jnp.where(masks[h], values.astype(F32), nothing).astype(BF)
 
-    tile = 128
+    tile = 256 if queries % 256 == 0 else 128
     scale = 1.0 / depth**0.5
-
-    def one_tile(i, carry):
-        rows = pl.ds(pl.multiple_of(i * tile, tile), tile)
-        scores = dot_t(qp[rows, :], ks[...])
-        d_probs = dot_t(dm[rows, :], vs[...])
+    for i in range(queries // tile):
+        cols = slice(i * tile, (i + 1) * tile)
+        scores = dot(ks[...], qp[:, cols])
+        d_probs = dot(vs[...], dm[:, cols])
         for h in range(HEADS):
             part = slice(h * anchors, (h + 1) * anchors)
-            s = scores[:, part] * scale
-            e = jnp.exp(s - jnp.max(s, axis=1, keepdims=True))
-            p = e / jnp.sum(e, axis=1, keepdims=True)
-            dp = d_probs[:, part]
-            d = p * (dp - jnp.sum(p * dp, axis=1, keepdims=True)) * scale
-            pm[rows, part] = p.astype(BF)
-            ds[rows, part] = d.astype(BF)
-        return carry
-
-    lax.fori_loop(0, queries // tile, one_tile, 0)
+            s = scores[part, :] * scale
+            e = jnp.exp(s - jnp.max(s, axis=0, keepdims=True))
+            p = e * (1.0 / jnp.sum(e, axis=0, keepdims=True))
+            dp = d_probs[part, :]
+            d = p * (dp - jnp.sum(p * dp, axis=0, keepdims=True)) * scale
+            pm[part, cols] = p.astype(BF)
+            ds[part, cols] = d.astype(BF)
 
     def own_heads(stacked):
         total = jnp.zeros((anchors, width), F32)
@@ -283,13 +277,13 @@
             total = jnp.where(masks[h], stacked[h * anchors:(h + 1) * anchors, :], total)
         return total.astype(BF).reshape(owners, a_here, width)
 
-    snd2[:, 0] = own_heads(dot_rows(ds[...], qp[...]))
-    snd2[:, 1] = own_heads(dot_rows(pm[...], dm[...]))
+    snd2[:, 0] = own_heads(dot_t(ds[...], qp[...]))
+    snd2[:, 1] = own_heads(dot_t(pm[...], dm[...]))
     rcv2[me] = snd2[me]
     exch[1].start(lambda to: snd2.at[to], lambda rank: rcv2.at[rank])
 
-    mixed = dot(pm[...], vs[...]).astype(BF)
-    attended[0] = dot(mixed, w_proj[...]).astype(BF)
+    mixed = dot_rows(vs[...], pm[...]).astype(BF)
+    attended[0] = dot_rows(w_proj[...], mixed).astype(BF)
     half_q = quads // 2
 
     def fill(ref, first, second, rows):
@@ -299,8 +293,8 @@
             ref[j, 0:rows, :] = src[k * rows:(k + 1) * rows, :].astype(BF)
 
     chunk = 2 * width // quads
-    d_query = dot(ds[...], ks[...]).astype(BF)
-    fill(r1a, dot_rows(mixed, cot[0]), dot_rows(qry[0], d_query), chunk)
+    d_query = dot_rows(ks[...], ds[...]).astype(BF)
+    fill(r1a, dot_t(mixed, cot[0]), dot_t(qry[0], d_query), chunk)
     red_pq.phase1()
 
     exch[1].wait_recv()
@@ -332,58 +326,71 @@
     own_number = own_o[:, 0:1] * float(a_here) + own_w[:, 0:1]
     own_member = jnp.where(own_number == own_lane, 1.0, 0.0).astype(BF)
     block_grad = dot(own_member, dpool[...].reshape(anchors, width)).astype(BF)
-    dhs[...] = dot_t(block_grad, w_out[...])
+    d_hidden = dot(block_grad, w_out[...])
     chunk_in = width // quads
     for j in range(quads):
         rows = slice(j * chunk_in, (j + 1) * chunk_in)
         total = jnp.zeros((chunk_in, hidden), F32)
         for b in range(blocks):
-            total = total + gmat[b, rows, :] * dhs[b:b + 1, :]
-        r3a[j] = total.astype(BF)
+            total = total + gmat[b, rows, :] * d_hidden[b:b + 1, :]
+        r3a[j, 0] = total.astype(BF)
+    hs_high, hs_low = two_parts(hs[...])
+    out_part = dot_rows(block_grad, hs_high) + dot_rows(block_grad, hs_low)
+    for j in range(quads):
+        r3a[j, 1] = out_part[j * chunk_in:(j + 1) * chunk_in, :].astype(BF)
     red_in.phase1()
-    out_part = dot_rows(hs_high, block_grad) + dot_rows(hs_low, block_grad)
-    for j in range(quads):
-        r4a[j] = out_part[j * chunk:(j + 1) * chunk, :].astype(BF)
-    red_out.phase1()
-
-    def one_back(b, carry):
-        rows = pl.ds(pl.multiple_of(b * rows_b, rows_b), rows_b)
-        d_pre = (gp[b].astype(F32) * dhs[pl.ds(b, 1), :]).astype(BF)
-        point_grad[0, rows, :] = dot_t(d_pre, w_in[...]).astype(BF)
-        return carry
-
+
+    turned = d_hidden.T
+
+    def back(first, last):
+        for i in range(first, last):
+            for b in range(i * wide_b, (i + 1) * wide_b):
+                cols = slice(b * rows_b, (b + 1) * rows_b)
+                gp[:, cols] = (gp[:, cols].astype(F32) * turned[:, b:b + 1]).astype(BF)
+            cols = slice(i * span, (i + 1) * span)
+            point_grad[0, :, cols] = dot(w_in[...], gp[:, cols]).astype(BF)
+
+    steps = blocks // wide_b
     red_kv.phase2()
-    lax.fori_loop(0, blocks // 2, one_back, 0)
+    back(0, steps // 2)
     red_in.phase2()
-    red_out.phase2()
     red_pq.phase3()
-    lax.fori_loop(blocks // 2, blocks, one_back, 0)
+    back(steps // 2, steps)
     red_kv.phase3()
     red_in.phase3()
-    red_out.phase3()
 
     red_pq.finish()
-    for j in range(quads):
-        ref = grad_proj if j < half_q else grad_query
-        k = j if j < half_q else j - half_q
-        ref[k * chunk:(k + 1) * chunk, :] = r1d[j].astype(F32)
+    fin_pq[...] = r1d[...]
     red_kv.finish()
-    for j in range(quads):
-        ref = grad_key if j < half_q else grad_value
-        k = j if j < half_q else j - half_q
-        ref[k * chunk:(k + 1) * chunk, :] = r2d[j, 0:chunk, :].astype(F32)
-    grad_gain[...] = r2d[0, chunk:, :].astype(F32)[0:1, :]
+    fin_kv[...] = r2d[...]
     red_in.finish()
-    for j in range(quads):
-        grad_in[j * chunk_in:(j + 1) * chunk_in, :] = r3d[j].astype(F32)
-    red_out.finish()
-    for j in range(quads):
-        grad_out[j * chunk:(j + 1) * chunk, :] = r4d[j].astype(F32)
+    fin_in[...] = r3d[...]
 
     for item in exch:
         item.wait_send()
-    for item in (red_pq, red_kv, red_in, red_out):
+    for item in (red_pq, red_kv, red_in):
         item.drain()
+
+
+def spread(
+    att_in, point_in, fin_in, fin_pq, fin_kv,
+    attended, point_grad, grad_in, grad_out, grad_query, grad_key, grad_value, grad_proj, grad_gain,
+):
+    attended[...] = att_in[...]
+    point_grad[...] = point_in[...]
+    quads = fin_in.shape[0]
+    half_q = quads // 2
+    rows_in = fin_in.shape[2]
+    chunk = fin_pq.shape[1]
+    for j in range(quads):
+        rows = slice(j * rows_in, (j + 1) * rows_in)
+        grad_in[rows, :] = fin_in[j, 0].astype(F32)
+        grad_out[rows, :] = fin_in[j, 1].astype(F32)
+        k = j % half_q
+        rows = slice(k * chunk, (k + 1) * chunk)
+        (grad_proj if j < half_q else grad_query)[rows, :] = fin_pq[j].astype(F32)
+        (grad_key if j < half_q else grad_value)[rows, :] = fin_kv[j, 0:chunk, :].astype(F32)
+    grad_gain[...] = fin_kv[0, chunk:, :].astype(F32)[0:1, :]
 
 
 def on_device(sizes, *args):
@@ -393,7 +400,7 @@
     width, hidden = w_in.shape
     blocks = assigned.shape[1]
     a_here = anchors.shape[1]
-    rows_b = points.shape[1] // blocks
+    n_pts = points.shape[1]
     slots = -(-blocks // 16) * 16
     lanes = -(-(width + 3) // 128) * 128
     n_q = queries.shape[1]
@@ -401,34 +408,37 @@
     chunk = 2 * width // quads
     chunk_in = width // quads
 
-    def red(rows, cols):
-        one = pltpu.VMEM((quads, rows, cols), BF)
-        return [one, one, pltpu.VMEM((n_z, rows, cols), BF), one]
+    def red(*shape):
+        one = pltpu.VMEM((quads, *shape), BF)
+        return [one, one, pltpu.VMEM((n_z, *shape), BF), one]
+
+    def turn(array):
+        return jnp.swapaxes(array, -1, -2)
 
     vmem = pl.BlockSpec(memory_space=pltpu.VMEM)
     smem = pl.BlockSpec(memory_space=pltpu.SMEM)
-    outs = pl.pallas_call(
+    firsts = pl.pallas_call(
         functools.partial(kernel, sizes),
         out_shape=[
-            jax.ShapeDtypeStruct(queries.shape, BF),
-            jax.ShapeDtypeStruct(points.shape, BF),
-            jax.ShapeDtypeStruct((width, hidden), F32),
-            jax.ShapeDtypeStruct((hidden, width), F32),
-            *[jax.ShapeDtypeStruct((width, width), F32)] * 4,
-            jax.ShapeDtypeStruct((1, width), F32),
+            jax.ShapeDtypeStruct((1, width, n_q), BF),
+            jax.ShapeDtypeStruct((1, width, n_pts), BF),
+            jax.ShapeDtypeStruct((quads, 2, chunk_in, hidden), BF),
+            jax.ShapeDtypeStruct((quads, chunk, width), BF),
+            jax.ShapeDtypeStruct((quads, chunk + 16, width), BF),
         ],
         in_specs=[vmem, smem] + [vmem] * 10,
-        out_specs=[vmem] * 9,
+        out_specs=[vmem] * 5,
         scratch_shapes=[
             pltpu.VMEM((slots, hidden), F32),
-            pltpu.VMEM((blocks, rows_b, hidden), BF),
+            pltpu.VMEM((hidden, n_pts), BF),
             pltpu.VMEM((blocks, width, hidden), F32),
-            pltpu.VMEM((hidden, lanes), BF),
+            pltpu.VMEM((hidden, width), BF),
+            pltpu.VMEM((lanes, hidden), BF),
             pltpu.VMEM((owners, slots + a_here, lanes), BF),
-            pltpu.VMEM((n_q, width), BF),
-            pltpu.VMEM((n_q, width), BF),
-            pltpu.VMEM((n_q, HEADS * total), BF),
-            pltpu.VMEM((n_q, HEADS * total), BF),
+            pltpu.VMEM((width, n_q), BF),
+            pltpu.VMEM((width, n_q), BF),
+            pltpu.VMEM((HEADS * total, n_q), BF),
+            pltpu.VMEM((HEADS * total, n_q), BF),
             pltpu.VMEM((HEADS * total, width), BF),
             pltpu.VMEM((HEADS * total, width), BF),
             pltpu.VMEM((total, width), F32),
@@ -436,21 +446,37 @@
             pltpu.VMEM((owners, 2, a_here, width), BF),
             pltpu.VMEM((owners, 2, a_here, width), BF),
             pltpu.VMEM((owners, a_here, width), BF),
-            pltpu.VMEM((slots, hidden), F32),
             *red(chunk, width),
             *red(chunk + 16, width),
-            *red(chunk_in, hidden),
-            *red(chunk, width),
+            *red(2, chunk_in, hidden),
             pltpu.SemaphoreType.DMA((6, owners)),
-            pltpu.SemaphoreType.DMA((16, quads)),
-            pltpu.SemaphoreType.DMA((8, n_z)),
+            pltpu.SemaphoreType.DMA((12, quads)),
+            pltpu.SemaphoreType.DMA((6, n_z)),
         ],
         compiler_params=pltpu.CompilerParams(
-            collective_id=0, has_side_effects=True, vmem_limit_bytes=56 * 1024 * 1024
+            collective_id=0, has_side_effects=True, vmem_limit_bytes=40 * 1024 * 1024
         ),
         name="layer",
-    )(points, assigned, anchors, queries, cotangent, gain.reshape(1, width), w_in, w_out, *squares)
-    return (*outs[:8], outs[8].reshape(width))
+    )(
+        turn(points), assigned, anchors, turn(queries), turn(cotangent),
+        gain.reshape(1, width), w_in, turn(w_out), *squares,
+    )
+    square = jax.ShapeDtypeStruct((width, width), F32)
+    both = jax.ShapeDtypeStruct((width, hidden), F32)
+    outs = pl.pallas_call(
+        spread,
+        out_shape=[
+            jax.ShapeDtypeStruct((1, width, n_q), BF),
+            jax.ShapeDtypeStruct((1, width, n_pts), BF),
+            both, both, square, square, square, square,
+            jax.ShapeDtypeStruct((1, width), F32),
+        ],
+        in_specs=[vmem] * 5,
+        out_specs=[vmem] * 9,
+        compiler_params=pltpu.CompilerParams(vmem_limit_bytes=16 * 1024 * 1024),
+        name="spread",
+    )(*firsts)
+    return (turn(outs[0]), turn(outs[1]), outs[2], turn(outs[3]), *outs[4:8], outs[8].reshape(width))
 
 
 def solution(mesh):

time: 62.7 us -> 51.7 us (0.82)
  local copies, waits for them, and re-layouts: 15.6 us -> 9.64 us
  Pallas kernels: 46.1 us -> 40.8 us
    pallas_call x1, Pallas kernels: 46.1 us -> 39.4 us  [on_device(): pl.pallas_call(functools.partial(kernel, sizes), out_shape=[jax.ShapeDtyp...]
    unnamed x31 -> x24, local copies, waits for them, and re-layouts: 15.6 us -> 9.64 us
    pallas_call x0 -> x1, Pallas kernels: none -> 1.45 us  [on_device(): pl.pallas_call(spread, out_shape=[jax.ShapeDtypeStruct((1, width, n_q), B...]
where the time goes in v2:
time: 51.7 us; the launch traced here: 51.2 us
  Pallas kernels  40.8 us (79%)
  local copies, waits for them, and re-layouts  9.64 us (19%)
  between operations  0.68 us (1%)
    pallas_call x1, Pallas kernels, on_device(): pl.pallas_call(functools.partial(kernel, sizes), out_shape=[jax.ShapeDtyp...  39.4 us
    unnamed x24, local copies, waits for them, and re-layouts  9.64 us
    pallas_call x1, Pallas kernels, on_device(): pl.pallas_call(spread, out_shape=[jax.ShapeDtypeStruct((1, width, n_q), B...  1.45 us

profile of v2, /device:TPU:0, one launch (start us, length us, event | category | flops | bytes accessed | tf_op | source)
XLA Modules:
  0.0 51.2 jit_solution(4058354999376585967)
XLA Ops:
  0.6 0.0 copy-start.9
  0.7 0.0 copy-start.10
  0.7 0.7 %copy-done.9 = bf16[1,16,192]{2,1,0:T(8,128)(2,1)S(1)} copy-done((bf16[1,16,192]{2,1,0:T(8,128)(2,1)S(1)}, bf16[1,16,192]{2,1,0:T(8,128)(2,1)}, u32[]{:S(2)}) %copy-start.9) | copy-done | bytes 6168
  1.3 0.0 copy-done.10
  1.3 0.0 copy-start
  1.3 1.1 %copy-done = bf16[1,1536,192]{1,2,0:T(8,128)(2,1)S(1)} copy-done((bf16[1,1536,192]{1,2,0:T(8,128)(2,1)S(1)}, bf16[1,1536,192]{1,2,0:T(8,128)(2,1)}, u32[]{:S(2)}) %copy-start) | copy-done | bytes 589848
  2.4 0.0 copy-start.1
  2.4 0.9 %copy-done.1 = bf16[1,512,192]{1,2,0:T(8,128)(2,1)S(1)} copy-done((bf16[1,512,192]{1,2,0:T(8,128)(2,1)S(1)}, bf16[1,512,192]{1,2,0:T(8,128)(2,1)}, u32[]{:S(2)}) %copy-start.1) | copy-done | bytes 196632
  3.3 0.0 copy-start.2
  3.3 0.9 %copy-done.2 = bf16[1,512,192]{1,2,0:T(8,128)(2,1)S(1)} copy-done((bf16[1,512,192]{1,2,0:T(8,128)(2,1)S(1)}, bf16[1,512,192]{1,2,0:T(8,128)(2,1)}, u32[]{:S(2)}) %copy-start.2) | copy-done | bytes 196632
  4.3 0.0 copy-start.3
  4.3 0.9 %copy-done.3 = bf16[192,384]{1,0:T(8,128)(2,1)S(1)} copy-done((bf16[192,384]{1,0:T(8,128)(2,1)S(1)}, bf16[192,384]{1,0:T(8,128)(2,1)}, u32[]{:S(2)}) %copy-start.3) | copy-done | bytes 147480
  5.2 0.0 copy-start.4
  5.2 0.9 %copy-done.4 = bf16[384,192]{0,1:T(8,128)(2,1)S(1)} copy-done((bf16[384,192]{0,1:T(8,128)(2,1)S(1)}, bf16[384,192]{0,1:T(8,128)(2,1)}, u32[]{:S(2)}) %copy-start.4) | copy-done | bytes 147480
  6.1 0.0 copy-start.5
  6.1 0.9 %copy-done.5 = bf16[192,192]{1,0:T(8,128)(2,1)S(1)} copy-done((bf16[192,192]{1,0:T(8,128)(2,1)S(1)}, bf16[192,192]{1,0:T(8,128)(2,1)}, u32[]{:S(2)}) %copy-start.5) | copy-done | bytes 73752
  7.0 0.0 copy-start.6
  7.0 0.9 %copy-done.6 = bf16[192,192]{1,0:T(8,128)(2,1)S(1)} copy-done((bf16[192,192]{1,0:T(8,128)(2,1)S(1)}, bf16[192,192]{1,0:T(8,128)(2,1)}, u32[]{:S(2)}) %copy-start.6) | copy-done | bytes 73752
  7.9 0.0 copy-start.7
  7.9 0.9 %copy-done.7 = bf16[192,192]{1,0:T(8,128)(2,1)S(1)} copy-done((bf16[192,192]{1,0:T(8,128)(2,1)S(1)}, bf16[192,192]{1,0:T(8,128)(2,1)}, u32[]{:S(2)}) %copy-start.7) | copy-done | bytes 73752
  8.8 0.0 copy-start.8
  8.8 0.9 %copy-done.8 = bf16[192,192]{1,0:T(8,128)(2,1)S(1)} copy-done((bf16[192,192]{1,0:T(8,128)(2,1)S(1)}, bf16[192,192]{1,0:T(8,128)(2,1)}, u32[]{:S(2)}) %copy-start.8) | copy-done | bytes 73752
  9.7 0.0 copy-start.11
  9.7 0.7 %copy-done.11 = s32[1,12]{1,0:T(1,128)S(1)} copy-done((s32[1,12]{1,0:T(1,128)S(1)}, s32[1,12]{1,0:T(1,128)}, u32[]{:S(2)}) %copy-start.11) | copy-done | bytes 72
  10.3 39.4 %layer.1 = (bf16[1,192,512]{2,1,0:T(8,128)(2,1)S(1)}, bf16[1,192,1536]{2,1,0:T(8,128)(2,1)S(1)}, bf16[4,2,48,384]{3,2,1,0:T(8,128)(2,1)S(1)}, bf16[4,96,192]{2,1,0:T(8,128)(2,1)S(1)}, bf16[4,112,192]{2,1,0:T(8,128)(2,1)S(1)}) custom-call(bf16[1,192,1536]{2,1,0:T(8,128)(2,1)S(1)} %bitcast.9, s32[1,12]{1,0:T(1,128)S(1)} %copy-done.11, ...), custom_call_target="tpu_custom_call" | custom-call | tf_op jit(solution)/shard_map/layer/pallas_call | solution.py:420
  49.7 1.5 %spread.1 = (bf16[1,192,512]{2,1,0:T(8,128)(2,1)}, bf16[1,192,1536]{2,1,0:T(8,128)(2,1)}, f32[192,384]{1,0:T(8,128)}, f32[192,384]{1,0:T(8,128)}, f32[192,192]{1...) custom-call(bf16[1,192,512]{2,1,0:T(8,128)(2,1)S(1)} %get-tuple-element.23.att_in,, ...), custom_call_target="tpu_custom_call" | custom-call | tf_op jit(solution)/shard_map/spread/pallas_call | solution.py:466
Async XLA Ops:
  0.6 0.7 %copy-start.9 = (bf16[1,16,192]{2,1,0:T(8,128)(2,1)S(1)}, bf16[1,16,192]{2,1,0:T(8,128)(2,1)}, u32[]{:S(2)}) copy-start(bf16[1,16,192]{2,1,0:T(8,128)(2,1)} %anc.1) | copy-start | bytes 18436
  0.7 0.7 %copy-start.10 = (f32[192]{0:T(256)S(1)}, f32[192]{0:T(256)}, u32[]{:S(2)}) copy-start(f32[192]{0:T(256)} %param.17) | copy-start | bytes 2308
  1.3 1.1 %copy-start = (bf16[1,1536,192]{1,2,0:T(8,128)(2,1)S(1)}, bf16[1,1536,192]{1,2,0:T(8,128)(2,1)}, u32[]{:S(2)}) copy-start(bf16[1,1536,192]{1,2,0:T(8,128)(2,1)} %param.12) | copy-start | bytes 1769476
  2.4 0.9 %copy-start.1 = (bf16[1,512,192]{1,2,0:T(8,128)(2,1)S(1)}, bf16[1,512,192]{1,2,0:T(8,128)(2,1)}, u32[]{:S(2)}) copy-start(bf16[1,512,192]{1,2,0:T(8,128)(2,1)} %param.15) | copy-start | bytes 589828
  3.3 0.9 %copy-start.2 = (bf16[1,512,192]{1,2,0:T(8,128)(2,1)S(1)}, bf16[1,512,192]{1,2,0:T(8,128)(2,1)}, u32[]{:S(2)}) copy-start(bf16[1,512,192]{1,2,0:T(8,128)(2,1)} %param.16) | copy-start | bytes 589828
  4.3 0.9 %copy-start.3 = (bf16[192,384]{1,0:T(8,128)(2,1)S(1)}, bf16[192,384]{1,0:T(8,128)(2,1)}, u32[]{:S(2)}) copy-start(bf16[192,384]{1,0:T(8,128)(2,1)} %w_in.1) | copy-start | bytes 442372
  5.2 0.9 %copy-start.4 = (bf16[384,192]{0,1:T(8,128)(2,1)S(1)}, bf16[384,192]{0,1:T(8,128)(2,1)}, u32[]{:S(2)}) copy-start(bf16[384,192]{0,1:T(8,128)(2,1)} %param.19) | copy-start | bytes 442372
  6.1 0.9 %copy-start.5 = (bf16[192,192]{1,0:T(8,128)(2,1)S(1)}, bf16[192,192]{1,0:T(8,128)(2,1)}, u32[]{:S(2)}) copy-start(bf16[192,192]{1,0:T(8,128)(2,1)} %w_query.1) | copy-start | bytes 221188
  7.0 0.9 %copy-start.6 = (bf16[192,192]{1,0:T(8,128)(2,1)S(1)}, bf16[192,192]{1,0:T(8,128)(2,1)}, u32[]{:S(2)}) copy-start(bf16[192,192]{1,0:T(8,128)(2,1)} %w_key.1) | copy-start | bytes 221188
  7.9 0.9 %copy-start.7 = (bf16[192,192]{1,0:T(8,128)(2,1)S(1)}, bf16[192,192]{1,0:T(8,128)(2,1)}, u32[]{:S(2)}) copy-start(bf16[192,192]{1,0:T(8,128)(2,1)} %w_value.1) | copy-start | bytes 221188
  8.8 0.9 %copy-start.8 = (bf16[192,192]{1,0:T(8,128)(2,1)S(1)}, bf16[192,192]{1,0:T(8,128)(2,1)}, u32[]{:S(2)}) copy-start(bf16[192,192]{1,0:T(8,128)(2,1)} %w_proj.1) | copy-start | bytes 221188
  9.7 0.7 %copy-start.11 = (s32[1,12]{1,0:T(1,128)S(1)}, s32[1,12]{1,0:T(1,128)}, u32[]{:S(2)}) copy-start(s32[1,12]{1,0:T(1,128)} %ids.1) | copy-start | bytes 148

commit v3 on v2

--- a/solution.py
+++ b/solution.py
@@ -113,14 +113,48 @@
         self.three.wait_send()
 
 
+class Cross:
+    def __init__(self, bufs, quad, across, cores, core, sems):
+        self.parts, self.got, self.final = bufs
+        self.q, self.x, self.cores, self.core = quad[0], across[0], cores, core
+        self.one = Exchange(*across, sems[0], sems[1])
+        self.two = Exchange(*quad, sems[2], sems[3])
+
+    def phase1(self):
+        self.got[self.x] = self.parts[self.q]
+        self.one.start(
+            lambda to: self.parts.at[to * self.cores + self.core], lambda me: self.got.at[me]
+        )
+
+    def phase2(self):
+        self.one.wait_recv()
+        self.final[self.q] = jnp.sum(self.got[...].astype(F32), axis=0).astype(BF)
+        q = self.q
+        self.two.start(lambda to: self.final.at[q], lambda me: self.final.at[me])
+
+    def finish(self):
+        self.two.wait_recv()
+
+    def drain(self):
+        self.one.wait_send()
+        self.two.wait_send()
+
+
 def kernel(
     sizes,
-    pts, ids, anc, qry, cot, gain, w_in, w_out, w_query, w_key, w_value, w_proj,
-    attended, point_grad, fin_in, fin_pq, fin_kv,
-    hs, gp, gmat, w_turned, w_pad, msg, qp, dm, pm, ds, ks, vs, asum, divs, snd2, rcv2, dpool,
-    r1a, r1b, r1c, r1d, r2a, r2b, r2c, r2d, r3a, r3b, r3c, r3d,
-    sem_o, sem_q, sem_z,
+    ids, *refs,
 ):
+    far, (attended, point_grad, fin_in, fin_pq, fin_x), near = refs[:11], refs[11:16], refs[16:27]
+    (
+        hs_all, gp, gmat, w_turned, w_pad, w_kv, msg, anc_all, qp, dm, pm, ds, ks, vs,
+        asum, divs, nrm, mem, snd2, rcv2, both_all,
+        r1a, r1b, r1c, r1d, r3a, r3b, r3c, r3d, r4a, r4b, r4d,
+        sem_in, sem_o, sem_q, sem_z, sem_x,
+    ) = refs[27:]
+    pts, anc, qry, cot, gain, w_in, w_out, w_query, w_key, w_value, w_proj = near
+    loads = [pltpu.make_async_copy(f, n, sem_in.at[i]) for i, (f, n) in enumerate(zip(far, near))]
+    for i in (5, 0, 6, 1, 2, 3, 7, 10, 4, 8, 9):
+        loads[i].start()
     n_z, n_x, n_c = sizes
     owners, quads = n_z * n_c, n_x * n_c
     z, x, c = lax.axis_index("geom"), lax.axis_index("design"), lax.axis_index("head")
@@ -131,7 +165,7 @@
     blocks = ids.shape[1]
     a_here = anc.shape[1]
     rows_b = pts.shape[2] // blocks
-    slots = msg.shape[1] - a_here
+    slots = msg.shape[1]
     anchors = owners * a_here
     queries = qry.shape[2]
     lanes = msg.shape[2]
@@ -148,7 +182,7 @@
     quad = (q, quads, quad_place)
     line = (z, n_z, line_place)
     exch = [
-        Exchange(me, owners, design_place, sem_o.at[2 * i], sem_o.at[2 * i + 1]) for i in range(3)
+        Exchange(me, owners, design_place, sem_o.at[2 * i], sem_o.at[2 * i + 1]) for i in range(5)
     ]
 
     def reducer(i, bufs):
@@ -157,8 +191,12 @@
         return Reduce((*bufs, sems), quad, line)
 
     red_pq = reducer(0, (r1a, r1b, r1c, r1d))
-    red_kv = reducer(1, (r2a, r2b, r2c, r2d))
-    red_in = reducer(2, (r3a, r3b, r3c, r3d))
+    red_in = reducer(1, (r3a, r3b, r3c, r3d))
+    across = (x, n_x, lambda to: {"design": to})
+    cross = Cross(
+        (r4a, r4b, r4d), quad, across, n_c, c,
+        (sem_x.at[0], sem_x.at[1], sem_q.at[8], sem_q.at[9]),
+    )
 
     barrier = pltpu.get_barrier_semaphore()
 
@@ -179,7 +217,13 @@
 
     c0 = 0.7978845608028654
     c1 = 0.044715 * c0
+    loads[5].wait()
     w_turned[...] = w_in[...].T
+    loads[1].wait()
+    anc_all[me] = anc[0]
+    pl.semaphore_wait(barrier, owners - 1 + (n_x - 1) * n_c)
+    exch[3].start(lambda to: anc_all.at[me], lambda rank: anc_all.at[rank])
+    loads[0].wait()
     wide_b = 2 if blocks % 2 == 0 else 1
     span = wide_b * rows_b
     span_row = lax.broadcasted_iota(jnp.int32, (slots, span), 0)
@@ -196,8 +240,8 @@
         hidden_sum = hidden_sum + dot_t(pick, hid)
         slope = half + 0.5 * pre * (1.0 - t * t) * (c0 + (3.0 * c1) * sq)
         gp[:, cols] = slope.astype(BF)
-    hs[...] = hidden_sum
-
+
+    loads[6].wait()
     w_pad[...] = jnp.zeros_like(w_pad)
     w_pad[0:width, :] = w_out[...]
     hs_high, hs_low = two_parts(hidden_sum)
@@ -216,34 +260,40 @@
     sums = jnp.where(lane == width, own_o, sums)
     sums = jnp.where(lane == width + 1, own_w, sums)
     sums = jnp.where(lane == width + 2, 1.0, sums)
-    msg[me, 0:slots, :] = sums.astype(BF)
-    msg[me, slots:, :] = jnp.zeros((a_here, lanes), BF)
-    msg[me, slots:, 0:width] = anc[0]
-
-    pl.semaphore_wait(barrier, owners - 1 + (n_x - 1) * n_c)
+    msg[me] = sums.astype(BF)
     exch[0].start(lambda to: msg.at[me], lambda rank: msg.at[rank])
-
+    hs_all[me] = hs_high
+    exch[4].start(lambda to: hs_all.at[me], lambda rank: hs_all.at[rank])
+
+    for i in (2, 3, 7, 10, 4, 8, 9):
+        loads[i].wait()
     qp[...] = dot_rows(w_query[...], qry[0]).astype(BF)
     dm[...] = dot(w_proj[...], cot[0]).astype(BF)
     for b in range(blocks):
         cols = slice(b * rows_b, (b + 1) * rows_b)
         gmat[b] = dot_t(pts[0, :, cols], gp[:, cols])
 
+    w_kv[:, 0:width] = w_key[...]
+    w_kv[:, width:] = w_value[...]
+
+    exch[3].wait_recv()
     exch[0].wait_recv()
-    arrived = msg[:, 0:slots, :].reshape(owners * slots, lanes)
+    arrived = msg[...].reshape(owners * slots, lanes)
     wide = arrived.astype(F32)
     numbers = wide[:, width:width + 1] * float(a_here) + wide[:, width + 1:width + 2]
     anchor_lane = lax.broadcasted_iota(jnp.int32, (owners * slots, anchors), 1).astype(F32)
     member = jnp.where(numbers == anchor_lane, 1.0, 0.0).astype(BF)
+    mem[...] = member
     pooled = dot_rows(member, arrived)
     divisor = jnp.maximum(pooled[:, width + 2:width + 3] * float(rows_b), 1.0)
-    anchor_rows = msg[:, slots:, 0:width].reshape(anchors, width).astype(F32)
+    anchor_rows = anc_all[...].reshape(anchors, width).astype(F32)
     anchor_sum = anchor_rows + pooled[:, 0:width] / divisor
     asum[...] = anchor_sum
     divs[...] = jnp.broadcast_to(divisor, divs.shape)
     gain_row = gain[...]
     inv_rms = lax.rsqrt(jnp.mean(anchor_sum * anchor_sum, axis=1, keepdims=True) + 1e-06)
     normed = (anchor_sum * inv_rms * gain_row).astype(BF)
+    nrm[...] = normed
     keys = dot(normed, w_key[...]).astype(BF)
     values = dot(normed, w_value[...]).astype(BF)
     depth = width // HEADS
@@ -275,10 +325,12 @@
         total = jnp.zeros((anchors, width), F32)
         for h in range(HEADS):
             total = jnp.where(masks[h], stacked[h * anchors:(h + 1) * anchors, :], total)
-        return total.astype(BF).reshape(owners, a_here, width)
-
-    snd2[:, 0] = own_heads(dot_t(ds[...], qp[...]))
-    snd2[:, 1] = own_heads(dot_t(pm[...], dm[...]))
+        return total
+
+    terms = jnp.concatenate(
+        [own_heads(dot_t(ds[...], qp[...])), own_heads(dot_t(pm[...], dm[...]))], axis=1
+    )
+    snd2[...] = terms.astype(BF).reshape(owners, a_here, 2 * width)
     rcv2[me] = snd2[me]
     exch[1].start(lambda to: snd2.at[to], lambda rank: rcv2.at[rank])
 
@@ -298,34 +350,24 @@
     red_pq.phase1()
 
     exch[1].wait_recv()
-    sum2 = jnp.sum(rcv2[...].astype(F32), axis=0).astype(BF)
-    key_grad, value_grad = sum2[0], sum2[1]
-    mine = pl.ds(pl.multiple_of(me * a_here, a_here), a_here)
-    a_sum = asum[mine, :]
-    div_own = divs[mine, 0:1]
+    both_all[me] = jnp.sum(rcv2[...].astype(F32), axis=0).astype(BF)
+    exch[2].start(lambda to: both_all.at[me], lambda rank: both_all.at[rank])
+    red_pq.phase2()
+
+    exch[2].wait_recv()
+    both = both_all[...].reshape(anchors, 2 * width)
+    a_sum = asum[...]
     inv = lax.rsqrt(jnp.mean(a_sum * a_sum, axis=1, keepdims=True) + 1e-06)
-    d_normed = dot_t(key_grad, w_key[...]) + dot_t(value_grad, w_value[...])
+    d_normed = dot_t(both, w_kv[...])
     scaled = d_normed * gain_row
     d_sum = inv * scaled - a_sum * (inv * inv * inv) * jnp.mean(
         scaled * a_sum, axis=1, keepdims=True
     )
-    dpool[me] = (d_sum / div_own).astype(BF)
-    exch[2].start(lambda to: dpool.at[me], lambda rank: dpool.at[rank])
-
-    gain_part = jnp.sum(d_normed * a_sum * inv, axis=0, keepdims=True)
-    own_normed = (a_sum * inv * gain_row).astype(BF)
-    fill(r2a, dot_rows(own_normed, key_grad), dot_rows(own_normed, value_grad), chunk)
-    extra = jnp.broadcast_to(gain_part, (r2a.shape[1] - chunk, width)).astype(BF)
-    for j in range(quads):
-        r2a[j, chunk:, :] = extra
-    red_kv.phase1()
-    red_pq.phase2()
-
-    exch[2].wait_recv()
+    d_pooled = (d_sum / divs[:, 0:1]).astype(BF)
     own_lane = lax.broadcasted_iota(jnp.int32, (slots, anchors), 1).astype(F32)
     own_number = own_o[:, 0:1] * float(a_here) + own_w[:, 0:1]
     own_member = jnp.where(own_number == own_lane, 1.0, 0.0).astype(BF)
-    block_grad = dot(own_member, dpool[...].reshape(anchors, width)).astype(BF)
+    block_grad = dot(own_member, d_pooled).astype(BF)
     d_hidden = dot(block_grad, w_out[...])
     chunk_in = width // quads
     for j in range(quads):
@@ -333,12 +375,21 @@
         total = jnp.zeros((chunk_in, hidden), F32)
         for b in range(blocks):
             total = total + gmat[b, rows, :] * d_hidden[b:b + 1, :]
-        r3a[j, 0] = total.astype(BF)
-    hs_high, hs_low = two_parts(hs[...])
-    out_part = dot_rows(block_grad, hs_high) + dot_rows(block_grad, hs_low)
+        r3a[j] = total.astype(BF)
+    red_in.phase1()
+    exch[4].wait_recv()
+    all_grads = dot(mem[...], d_pooled).astype(BF)
+    out_part = dot_rows(all_grads, hs_all[...].reshape(owners * slots, hidden)).astype(BF)
+    both_part = dot_rows(nrm[...], both).astype(BF)
+    gain_part = jnp.sum(d_normed * a_sum * inv, axis=0, keepdims=True)
+    gain_rows = jnp.broadcast_to(gain_part, (16, width)).astype(BF)
+    r4a[:, 2 * chunk_in:, :] = jnp.zeros((quads, 16, hidden), BF)
     for j in range(quads):
-        r3a[j, 1] = out_part[j * chunk_in:(j + 1) * chunk_in, :].astype(BF)
-    red_in.phase1()
+        rows = slice(j * chunk_in, (j + 1) * chunk_in)
+        r4a[j, 0:chunk_in, :] = out_part[rows, :]
+        r4a[j, chunk_in:2 * chunk_in, :] = both_part[rows, :]
+        r4a[j, 2 * chunk_in:, 0:width] = gain_rows
+    cross.phase1()
 
     turned = d_hidden.T
 
@@ -351,46 +402,48 @@
             point_grad[0, :, cols] = dot(w_in[...], gp[:, cols]).astype(BF)
 
     steps = blocks // wide_b
-    red_kv.phase2()
     back(0, steps // 2)
     red_in.phase2()
+    cross.phase2()
     red_pq.phase3()
     back(steps // 2, steps)
-    red_kv.phase3()
     red_in.phase3()
 
+    cross.finish()
+    fin_x[...] = r4d[...]
     red_pq.finish()
     fin_pq[...] = r1d[...]
-    red_kv.finish()
-    fin_kv[...] = r2d[...]
     red_in.finish()
     fin_in[...] = r3d[...]
 
     for item in exch:
         item.wait_send()
-    for item in (red_pq, red_kv, red_in):
+    for item in (red_pq, red_in, cross):
         item.drain()
 
 
 def spread(
-    att_in, point_in, fin_in, fin_pq, fin_kv,
+    att_in, point_in, fin_in, fin_pq, fin_x,
     attended, point_grad, grad_in, grad_out, grad_query, grad_key, grad_value, grad_proj, grad_gain,
 ):
     attended[...] = att_in[...]
     point_grad[...] = point_in[...]
     quads = fin_in.shape[0]
     half_q = quads // 2
-    rows_in = fin_in.shape[2]
+    rows_in = fin_in.shape[1]
     chunk = fin_pq.shape[1]
+    width = fin_pq.shape[2]
     for j in range(quads):
         rows = slice(j * rows_in, (j + 1) * rows_in)
-        grad_in[rows, :] = fin_in[j, 0].astype(F32)
-        grad_out[rows, :] = fin_in[j, 1].astype(F32)
+        grad_in[rows, :] = fin_in[j].astype(F32)
+        grad_out[rows, :] = fin_x[j, 0:rows_in, :].astype(F32)
+        pair = fin_x[j, rows_in:2 * rows_in, :].astype(F32)
+        grad_key[rows, :] = pair[:, 0:width]
+        grad_value[rows, :] = pair[:, width:]
         k = j % half_q
         rows = slice(k * chunk, (k + 1) * chunk)
         (grad_proj if j < half_q else grad_query)[rows, :] = fin_pq[j].astype(F32)
-        (grad_key if j < half_q else grad_value)[rows, :] = fin_kv[j, 0:chunk, :].astype(F32)
-    grad_gain[...] = fin_kv[0, chunk:, :].astype(F32)[0:1, :]
+    grad_gain[...] = fin_x[0, 2 * rows_in:, :].astype(F32)[0:1, 0:width]
 
 
 def on_device(sizes, *args):
@@ -415,6 +468,10 @@
     def turn(array):
         return jnp.swapaxes(array, -1, -2)
 
+    operands = [
+        turn(points), anchors, turn(queries), turn(cotangent),
+        gain.reshape(1, width), w_in, turn(w_out), *squares,
+    ]
     vmem = pl.BlockSpec(memory_space=pltpu.VMEM)
     smem = pl.BlockSpec(memory_space=pltpu.SMEM)
     firsts = pl.pallas_call(
@@ -422,19 +479,22 @@
         out_shape=[
             jax.ShapeDtypeStruct((1, width, n_q), BF),
             jax.ShapeDtypeStruct((1, width, n_pts), BF),
-            jax.ShapeDtypeStruct((quads, 2, chunk_in, hidden), BF),
+            jax.ShapeDtypeStruct((quads, chunk_in, hidden), BF),
             jax.ShapeDtypeStruct((quads, chunk, width), BF),
-            jax.ShapeDtypeStruct((quads, chunk + 16, width), BF),
+            jax.ShapeDtypeStruct((quads, 2 * chunk_in + 16, hidden), BF),
         ],
-        in_specs=[vmem, smem] + [vmem] * 10,
+        in_specs=[smem] + [pl.BlockSpec(memory_space=pltpu.HBM)] * 11,
         out_specs=[vmem] * 5,
         scratch_shapes=[
-            pltpu.VMEM((slots, hidden), F32),
+            *[pltpu.VMEM(item.shape, item.dtype) for item in operands],
+            pltpu.VMEM((owners, slots, hidden), BF),
             pltpu.VMEM((hidden, n_pts), BF),
             pltpu.VMEM((blocks, width, hidden), F32),
             pltpu.VMEM((hidden, width), BF),
             pltpu.VMEM((lanes, hidden), BF),
-            pltpu.VMEM((owners, slots + a_here, lanes), BF),
+            pltpu.VMEM((width, 2 * width), BF),
+            pltpu.VMEM((owners, slots, lanes), BF),
+            pltpu.VMEM((owners, a_here, width), BF),
             pltpu.VMEM((width, n_q), BF),
             pltpu.VMEM((width, n_q), BF),
             pltpu.VMEM((HEADS * total, n_q), BF),
@@ -443,24 +503,27 @@
             pltpu.VMEM((HEADS * total, width), BF),
             pltpu.VMEM((total, width), F32),
             pltpu.VMEM((total, 128), F32),
-            pltpu.VMEM((owners, 2, a_here, width), BF),
-            pltpu.VMEM((owners, 2, a_here, width), BF),
-            pltpu.VMEM((owners, a_here, width), BF),
+            pltpu.VMEM((total, width), BF),
+            pltpu.VMEM((owners * slots, total), BF),
+            pltpu.VMEM((owners, a_here, 2 * width), BF),
+            pltpu.VMEM((owners, a_here, 2 * width), BF),
+            pltpu.VMEM((owners, a_here, 2 * width), BF),
             *red(chunk, width),
-            *red(chunk + 16, width),
-            *red(2, chunk_in, hidden),
-            pltpu.SemaphoreType.DMA((6, owners)),
-            pltpu.SemaphoreType.DMA((12, quads)),
-            pltpu.SemaphoreType.DMA((6, n_z)),
+            *red(chunk_in, hidden),
+            pltpu.VMEM((quads, 2 * chunk_in + 16, hidden), BF),
+            pltpu.VMEM((n_x, 2 * chunk_in + 16, hidden), BF),
+            pltpu.VMEM((quads, 2 * chunk_in + 16, hidden), BF),
+            pltpu.SemaphoreType.DMA((11,)),
+            pltpu.SemaphoreType.DMA((10, owners)),
+            pltpu.SemaphoreType.DMA((10, quads)),
+            pltpu.SemaphoreType.DMA((4, n_z)),
+            pltpu.SemaphoreType.DMA((2, n_x)),
         ],
         compiler_params=pltpu.CompilerParams(
-            collective_id=0, has_side_effects=True, vmem_limit_bytes=40 * 1024 * 1024
+            collective_id=0, has_side_effects=True, vmem_limit_bytes=63 * 1024 * 1024
         ),
         name="layer",
-    )(
-        turn(points), assigned, anchors, turn(queries), turn(cotangent),
-        gain.reshape(1, width), w_in, turn(w_out), *squares,
-    )
+    )(assigned, *operands)
     square = jax.ShapeDtypeStruct((width, width), F32)
     both = jax.ShapeDtypeStruct((width, hidden), F32)
     outs = pl.pallas_call(
@@ -473,7 +536,7 @@
         ],
         in_specs=[vmem] * 5,
         out_specs=[vmem] * 9,
-        compiler_params=pltpu.CompilerParams(vmem_limit_bytes=16 * 1024 * 1024),
+        compiler_params=pltpu.CompilerParams(vmem_limit_bytes=63 * 1024 * 1024),
         name="spread",
     )(*firsts)
     return (turn(outs[0]), turn(outs[1]), outs[2], turn(outs[3]), *outs[4:8], outs[8].reshape(width))

time: 51.7 us -> 43.8 us (0.85)
  the two profiles are of different devices: /device:TPU:0 before, /device:TPU:15 now
where the time goes in v3:
time: 43.8 us; the launch traced here: 43.7 us
  Pallas kernels  43 us (98%)
  between operations  0.65 us (1%)
    pallas_call x1, Pallas kernels, on_device(): pl.pallas_call(functools.partial(kernel, sizes), out_shape=[jax.ShapeDtyp...  40.4 us
    pallas_call x1, Pallas kernels, on_device(): pl.pallas_call(spread, out_shape=[jax.ShapeDtypeStruct((1, width, n_q), B...  2.67 us

profile of v3, /device:TPU:15, one launch (start us, length us, event | category | flops | bytes accessed | tf_op | source)
XLA Modules:
  0.0 43.7 jit_solution(14959169147558647912)
XLA Ops:
  0.6 40.4 %layer.1 = (bf16[1,192,512]{2,1,0:T(8,128)(2,1)}, bf16[1,192,1536]{2,1,0:T(8,128)(2,1)}, bf16[4,48,384]{2,1,0:T(8,128)(2,1)}, bf16[4,96,192]{2,1,0:T(8,128)(2,1)}, bf16[4,112,384]{2,1,0:T(8,128)(2,1)}) custom-call(s32[1,12]{1,0:T(1,128)} %ids.1, bf16[1,192,1536]{2,1,0:T(8,128)(2,1)} %bitcast.9, bf16[1,16,192]{2,1,0:T(8,128)(2,1)} %refs_1_.1, ...), custom_call_target="tpu_custom_call" | custom-call | tf_op jit(solution)/shard_map/layer/pallas_call | solution.py:477
  41.0 2.7 %spread.1 = (bf16[1,192,512]{2,1,0:T(8,128)(2,1)}, bf16[1,192,1536]{2,1,0:T(8,128)(2,1)}, f32[192,384]{1,0:T(8,128)}, f32[192,384]{1,0:T(8,128)}, f32[192,192]{1...) custom-call(bf16[1,192,512]{2,1,0:T(8,128)(2,1)} %get-tuple-element.23.att_in, ...), custom_call_target="tpu_custom_call" | custom-call | tf_op jit(solution)/shard_map/spread/pallas_call | solution.py:529

commit v4 on v3

--- a/solution.py
+++ b/solution.py
@@ -336,17 +336,11 @@
 
     mixed = dot_rows(vs[...], pm[...]).astype(BF)
     attended[0] = dot_rows(w_proj[...], mixed).astype(BF)
-    half_q = quads // 2
-
-    def fill(ref, first, second, rows):
-        for j in range(quads):
-            src = first if j < half_q else second
-            k = j if j < half_q else j - half_q
-            ref[j, 0:rows, :] = src[k * rows:(k + 1) * rows, :].astype(BF)
-
-    chunk = 2 * width // quads
     d_query = dot_rows(ks[...], ds[...]).astype(BF)
-    fill(r1a, dot_t(mixed, cot[0]), dot_t(qry[0], d_query), chunk)
+    pair = jnp.concatenate([dot_t(mixed, cot[0]), dot_t(qry[0], d_query)], axis=1).astype(BF)
+    chunk_in = width // quads
+    for j in range(quads):
+        r1a[j] = pair[j * chunk_in:(j + 1) * chunk_in, :]
     red_pq.phase1()
 
     exch[1].wait_recv()
@@ -369,7 +363,6 @@
     own_member = jnp.where(own_number == own_lane, 1.0, 0.0).astype(BF)
     block_grad = dot(own_member, d_pooled).astype(BF)
     d_hidden = dot(block_grad, w_out[...])
-    chunk_in = width // quads
     for j in range(quads):
         rows = slice(j * chunk_in, (j + 1) * chunk_in)
         total = jnp.zeros((chunk_in, hidden), F32)
@@ -429,10 +422,8 @@
     attended[...] = att_in[...]
     point_grad[...] = point_in[...]
     quads = fin_in.shape[0]
-    half_q = quads // 2
     rows_in = fin_in.shape[1]
-    chunk = fin_pq.shape[1]
-    width = fin_pq.shape[2]
+    width = grad_key.shape[1]
     for j in range(quads):
         rows = slice(j * rows_in, (j + 1) * rows_in)
         grad_in[rows, :] = fin_in[j].astype(F32)
@@ -440,9 +431,9 @@
         pair = fin_x[j, rows_in:2 * rows_in, :].astype(F32)
         grad_key[rows, :] = pair[:, 0:width]
         grad_value[rows, :] = pair[:, width:]
-        k = j % half_q
-        rows = slice(k * chunk, (k + 1) * chunk)
-        (grad_proj if j < half_q else grad_query)[rows, :] = fin_pq[j].astype(F32)
+        pair = fin_pq[j].astype(F32)
+        grad_proj[rows, :] = pair[:, 0:width]
+        grad_query[rows, :] = pair[:, width:]
     grad_gain[...] = fin_x[0, 2 * rows_in:, :].astype(F32)[0:1, 0:width]
 
 
@@ -458,7 +449,6 @@
     lanes = -(-(width + 3) // 128) * 128
     n_q = queries.shape[1]
     total = owners * a_here
-    chunk = 2 * width // quads
     chunk_in = width // quads
 
     def red(*shape):
@@ -480,7 +470,7 @@
             jax.ShapeDtypeStruct((1, width, n_q), BF),
             jax.ShapeDtypeStruct((1, width, n_pts), BF),
             jax.ShapeDtypeStruct((quads, chunk_in, hidden), BF),
-            jax.ShapeDtypeStruct((quads, chunk, width), BF),
+            jax.ShapeDtypeStruct((quads, chunk_in, 2 * width), BF),
             jax.ShapeDtypeStruct((quads, 2 * chunk_in + 16, hidden), BF),
         ],
         in_specs=[smem] + [pl.BlockSpec(memory_space=pltpu.HBM)] * 11,
@@ -508,7 +498,7 @@
             pltpu.VMEM((owners, a_here, 2 * width), BF),
             pltpu.VMEM((owners, a_here, 2 * width), BF),
             pltpu.VMEM((owners, a_here, 2 * width), BF),
-            *red(chunk, width),
+            *red(chunk_in, 2 * width),
             *red(chunk_in, hidden),
             pltpu.VMEM((quads, 2 * chunk_in + 16, hidden), BF),
             pltpu.VMEM((n_x, 2 * chunk_in + 16, hidden), BF),

time: 43.8 us -> 42.8 us (0.977)
  the two profiles are of different devices: /device:TPU:15 before, /device:TPU:0 now
where the time goes in v4:
time: 42.8 us; the launch traced here: 42.4 us
  Pallas kernels  41.7 us (97%)
  between operations  0.65 us (2%)
    pallas_call x1, Pallas kernels, on_device(): pl.pallas_call(functools.partial(kernel, sizes), out_shape=[jax.ShapeDtyp...  39.1 us
    pallas_call x1, Pallas kernels, on_device(): pl.pallas_call(spread, out_shape=[jax.ShapeDtypeStruct((1, width, n_q), B...  2.67 us

profile of v4, /device:TPU:0, one launch (start us, length us, event | category | flops | bytes accessed | tf_op | source)
XLA Modules:
  0.0 42.4 jit_solution(1528462421034640517)
XLA Ops:
  0.6 39.1 %layer.1 = (bf16[1,192,512]{2,1,0:T(8,128)(2,1)}, bf16[1,192,1536]{2,1,0:T(8,128)(2,1)}, bf16[4,48,384]{2,1,0:T(8,128)(2,1)}, bf16[4,48,384]{2,1,0:T(8,128)(2,1)}, bf16[4,112,384]{2,1,0:T(8,128)(2,1)}) custom-call(s32[1,12]{1,0:T(1,128)} %ids.1, bf16[1,192,1536]{2,1,0:T(8,128)(2,1)} %bitcast.9, bf16[1,16,192]{2,1,0:T(8,128)(2,1)} %refs_1_.1, ...), custom_call_target="tpu_custom_call" | custom-call | tf_op jit(solution)/shard_map/layer/pallas_call | solution.py:467
  39.7 2.7 %spread.1 = (bf16[1,192,512]{2,1,0:T(8,128)(2,1)}, bf16[1,192,1536]{2,1,0:T(8,128)(2,1)}, f32[192,384]{1,0:T(8,128)}, f32[192,384]{1,0:T(8,128)}, f32[192,192]{1...) custom-call(bf16[1,192,512]{2,1,0:T(8,128)(2,1)} %get-tuple-element.23.att_in, ...), custom_call_target="tpu_custom_call" | custom-call | tf_op jit(solution)/shard_map/spread/pallas_call | solution.py:519
